TPU v7x, 32 devices: a whole 2x2x4 slice. The times are simulated.
32 devices in a mesh: wide: 16 (over z, x, core), narrow: 2 (over y).
Axes of the slice: x: 2, y: 2, z: 4, core: 2. Of those that a mesh axis runs over, the one named last changes fastest.
Arguments:
- dosage: bfloat16 [2048, 32768], P(None, 'wide'), may hold values from -4 to 6, as said below
- annotations: int32 [128, 32768], P(None, 'wide'), may hold values from 0 to 1, as said below
- test_statistic_table: float32 [32768, 512], P('wide', 'narrow'), may hold values from 0 to 200
Outputs:
- ld_scores: float32 [128, 32768], P(None, ('wide', 'narrow'))
- fitted: float32 [32768, 512], P('wide', 'narrow')
Inputs may be any that keep to these rules, and one draw needn't show every extreme that they name: `dosage`: dosages of each variant follow a correlated process along the variants. `annotations`: 1 where a variant belongs to an annotation.
All inputs are finite; a program needn't handle non-finite values.
Results may differ from a plain program's by a relative error of at most 0.0023.
Values may be sent and summed in bfloat16 or wider, within the bound.
No kernel may reach another device: no remote copies, remote signals or barrier semaphores. Data moves between devices by JAX's collectives and lax.ppermute only.
A program may use at most 128 MiB of HBM per device.

v0:
```python
import functools

import jax
import jax.numpy as jnp
from jax import lax
from jax.experimental import pallas as pl
from jax.experimental.pallas import tpu as pltpu
from jax.sharding import PartitionSpec as P


EPS = 1e-05
TILE = 256
LANES = 128
ROWS = 64
PAD = 8
PIVOTS = 4
VMEM_LIMIT = 16 * 1024 * 1024

highest_precision = lax.Precision.HIGHEST
both = ("wide", "narrow")
in_vmem = pl.BlockSpec(memory_space=pltpu.VMEM)
in_place = pl.BlockSpec(memory_space=pl.ANY)
in_smem = pl.BlockSpec(memory_space=pltpu.SMEM)


def cols_at(c):
    return pl.ds(pl.multiple_of(c * TILE, TILE), TILE)


def standardized(read, write, wide_values, samples):
    steps = samples // ROWS
    pivot = read(pl.ds(0, 2 * PAD)).astype(jnp.float32)[:1, :]

    def folded(values):
        return jnp.sum(values.reshape(-1, 4 * PAD, TILE), axis=0)

    first = second = jnp.zeros((4 * PAD, TILE), jnp.float32)
    for r in range(steps):
        rows = pl.ds(r * ROWS, ROWS)
        values = read(rows).astype(jnp.float32) - pivot
        wide_values[rows, :] = values
        first, second = first + folded(values), second + folded(values * values)
    first, second = (
        jnp.sum(value, axis=0, keepdims=True) / samples for value in (first, second)
    )
    variance = jnp.maximum(second - first * first, 0.0)
    scale = 1.0 / jnp.sqrt(variance + EPS)
    for r in range(steps):
        rows = pl.ds(r * ROWS, ROWS)
        write(rows, ((wide_values[rows, :] - first) * scale).astype(jnp.bfloat16))


def into(geno, tile):
    def write(rows, value):
        geno[2 * tile, rows, :] = value[:, :LANES]
        geno[2 * tile + 1, rows, :] = value[:, LANES:]

    return write


def columns_of(geno, tile):
    return jnp.concatenate([geno[2 * tile], geno[2 * tile + 1]], axis=1)


def rows_of(turned, tile):
    return jnp.concatenate([turned[tile, k] for k in range(turned.shape[1])], axis=1)


def band_weights(rows, columns, inside=None):
    samples = rows.shape[1]
    products = jnp.dot(rows, columns, preferred_element_type=jnp.float32)
    unit = 1.0 / (samples - 2)
    weights = products * products * ((1.0 + unit) / (samples * samples)) - unit
    if inside is not None:
        weights = jnp.where(inside, weights, 0.0)
    return weights.astype(jnp.bfloat16)


def along_rows(annot, weights):
    return jnp.dot(annot, weights, preferred_element_type=jnp.float32)


def along_columns(annot, weights):
    return lax.dot_general(
        annot, weights, (((1,), (1,)), ((), ())), preferred_element_type=jnp.float32
    )


def tile_offset():
    shape = (TILE, TILE)
    return lax.broadcasted_iota(jnp.int32, shape, 0) - lax.broadcasted_iota(jnp.int32, shape, 1)


def sizes(dosage):
    samples, strip = dosage.shape
    return samples, strip, strip // (2 * TILE)


def outgoing_kernel(n_ref, dosage_ref, annot_ref, first_ref, second_ref, given_annot, came):
    samples, strip = dosage_ref.shape
    annots = annot_ref.shape[0]
    n = n_ref[0]
    outs = (first_ref, second_ref)
    copies = []
    for order, out_ref in enumerate(outs):
        column = cols_at((1 - n) * (strip // TILE - 1 - order) + n * order)
        copies += [
            pltpu.make_async_copy(
                dosage_ref.at[:, column], out_ref.at[:samples, :], came.at[2 * order]
            ),
            pltpu.make_async_copy(
                annot_ref.at[:, column], given_annot.at[order], came.at[2 * order + 1]
            ),
        ]
    for copy in copies:
        copy.start()
    row = lax.broadcasted_iota(jnp.int32, (PAD, TILE), 0)
    for order, out_ref in enumerate(outs):
        out_ref[samples + annots :, :] = jnp.where(row == 0, 1.0, 0.0).astype(jnp.bfloat16)
        copies[2 * order + 1].wait()
        out_ref[samples : samples + annots, :] = (
            given_annot[order].astype(jnp.float32).astype(jnp.bfloat16)
        )
    for order in range(2):
        copies[2 * order].wait()


def outgoing_columns(n, dosage, annotations):
    samples = dosage.shape[0]
    annots = annotations.shape[0]
    out = jax.ShapeDtypeStruct((samples + annots + PAD, TILE), jnp.bfloat16)
    return pl.pallas_call(
        outgoing_kernel,
        out_shape=(out, out),
        in_specs=[in_smem, in_place, in_place],
        out_specs=(in_vmem, in_vmem),
        scratch_shapes=[pltpu.VMEM((2, annots, TILE), jnp.int32), pltpu.SemaphoreType.DMA((4,))],
        cost_estimate=pl.CostEstimate(
            flops=0, bytes_accessed=8 * samples * TILE, transcendentals=0
        ),
        name="outgoing",
    )(n, dosage, annotations)


def prepare_kernel(n_ref, annot_ref, chi_ref, annot_out_ref, counts_ref, chi_out_ref, came):
    annots, strip = annot_ref.shape
    block = strip // 2
    n = n_ref[0]
    rows = pl.ds(pl.multiple_of((1 - n) * block, block), block)
    copy = pltpu.make_async_copy(chi_ref.at[rows, :], chi_out_ref, came)
    copy.start()
    row = lax.broadcasted_iota(jnp.int32, (PAD, strip), 0)
    annot_out_ref[annots:, :] = jnp.where(row == 0, 1.0, 0.0).astype(jnp.bfloat16)
    members = annot_ref[...].astype(jnp.float32)
    annot_out_ref[:annots, :] = members.astype(jnp.bfloat16)
    counts_ref[...] = lying(jnp.sum(members, axis=1, keepdims=True))
    copy.wait()


def prepared(n, annotations, chi):
    annots, strip = annotations.shape
    return pl.pallas_call(
        prepare_kernel,
        out_shape=(
            jax.ShapeDtypeStruct((annots + PAD, strip), jnp.bfloat16),
            jax.ShapeDtypeStruct((1, annots), jnp.float32),
            jax.ShapeDtypeStruct((strip // 2, chi.shape[1]), jnp.float32),
        ),
        in_specs=[in_smem, in_vmem, in_place],
        out_specs=(in_vmem,) * 3,
        scratch_shapes=[pltpu.SemaphoreType.DMA],
        compiler_params=pltpu.CompilerParams(vmem_limit_bytes=VMEM_LIMIT),
        cost_estimate=pl.CostEstimate(
            flops=0, bytes_accessed=16 * strip * annots, transcendentals=0
        ),
        name="prepare",
    )(n, annotations, chi)


def own_kernel(n_ref, dosage_ref, annot_ref, sums_ref, turned_ref, geno, wide_values):
    samples, strip = dosage_ref.shape
    mine = strip // (2 * TILE)
    n = n_ref[0]
    sums_ref[...] = jnp.zeros_like(sums_ref)

    def standardize(t):
        standardized(
            lambda rows: dosage_ref[rows, cols_at(n * mine + t)],
            into(geno, t),
            wide_values.at[t % 2],
            samples,
        )
        for k in range(samples // LANES):
            for part in range(2):
                turned_ref[t, k, part * LANES : (part + 1) * LANES, :] = geno[
                    2 * t + part, k * LANES : (k + 1) * LANES, :
                ].T

    standardize(0)
    for y in range(mine):
        if y + 1 < mine:
            standardize(y + 1)
        for x in range(y + 1):
            weights = band_weights(rows_of(turned_ref, x), columns_of(geno, y))
            sums_ref[:, y * TILE : (y + 1) * TILE] += along_rows(
                annot_ref[:, cols_at(n * mine + x)], weights
            )
            if x < y:
                sums_ref[:, x * TILE : (x + 1) * TILE] += along_columns(
                    annot_ref[:, cols_at(n * mine + y)], weights
                )


def other_kernel(
    slots, n_ref, dosage_ref, annot_ref, turned_ref, sums_in, sums_ref, geno, wide_values
):
    samples, strip = dosage_ref.shape
    mine = strip // (2 * TILE)
    n = n_ref[0]

    def nearest(s):
        return (1 - n) * s + n * (mine - 1 - s)

    sums_ref[...] = sums_in[...]
    inside = (1 - 2 * n) * tile_offset() >= 0

    def standardize(s):
        standardized(
            lambda rows: dosage_ref[rows, cols_at((1 - n) * mine + nearest(s))],
            into(geno, s),
            wide_values.at[s % 2],
            samples,
        )

    standardize(slots[0])
    for s in slots:
        if s + 1 in slots:
            standardize(s + 1)
        for h in range(s, mine):
            weights = band_weights(
                rows_of(turned_ref, nearest(h)), columns_of(geno, s), inside if h == s else None
            )
            sums_ref[:, cols_at(nearest(h))] += along_columns(
                annot_ref[:, cols_at((1 - n) * mine + nearest(s))], weights
            )


def own_sums(n, dosage, annot):
    samples, strip, mine = sizes(dosage)
    chunks = samples // LANES
    turned = (mine, chunks, TILE, LANES)
    return pl.pallas_call(
        own_kernel,
        out_shape=(
            jax.ShapeDtypeStruct((annot.shape[0], strip // 2), jnp.float32),
            jax.ShapeDtypeStruct(turned, jnp.bfloat16),
        ),
        in_specs=[in_smem, in_vmem, in_vmem],
        out_specs=(in_vmem, in_vmem),
        scratch_shapes=strip_scratch(dosage),
        cost_estimate=strip_cost(dosage),
        compiler_params=pltpu.CompilerParams(vmem_limit_bytes=VMEM_LIMIT),
        name="own_sums",
    )(n, dosage, annot)


def other_sums(slots, n, dosage, annot, turned, sums):
    return pl.pallas_call(
        functools.partial(other_kernel, slots),
        out_shape=jax.ShapeDtypeStruct(sums.shape, jnp.float32),
        in_specs=[in_smem] + [in_vmem] * 4,
        out_specs=in_vmem,
        scratch_shapes=strip_scratch(dosage),
        cost_estimate=strip_cost(dosage),
        compiler_params=pltpu.CompilerParams(vmem_limit_bytes=VMEM_LIMIT),
        name="other_sums",
    )(n, dosage, annot, turned, sums)


def strip_scratch(dosage):
    samples, _, mine = sizes(dosage)
    return [
        pltpu.VMEM((2 * mine, samples, LANES), jnp.bfloat16),
        pltpu.VMEM((2, samples, TILE), jnp.float32),
    ]


def strip_cost(dosage):
    samples, strip, _ = sizes(dosage)
    return pl.CostEstimate(
        flops=samples * strip * strip // 2, bytes_accessed=2 * samples * strip, transcendentals=0
    )


def rim_kernel(
    order, n_ref, arrived_ref, turned_ref, annot_ref, sums_in, sums_ref, back_ref, geno, wide_values
):
    mine = turned_ref.shape[0]
    samples = geno.shape[1]
    n = n_ref[0]
    sums_ref[...] = sums_in[...]
    back_ref[...] = jnp.zeros_like(back_ref)
    standardized(lambda rows: arrived_ref[rows, :], into(geno, 0), wide_values, samples)

    def add(y, inside=None):
        weights = band_weights(rows_of(turned_ref, y), columns_of(geno, 0), inside)
        sums_ref[:, cols_at(y)] += along_columns(arrived_ref[samples:, :], weights)
        back_ref[...] += along_rows(annot_ref[:, cols_at(n * mine + y)], weights)

    low, high = order, mine - 1 - order
    add((1 - n) * high + n * low, (1 - 2 * n) * tile_offset() <= 0)
    width, last = mine // 2, mine - mine // 4
    for y in range(mine):
        first = y < high and (y >= width or high >= last)
        second = low < y < last
        if first or second:

            @pl.when(True if first and second else (n == 0 if first else n == 1))
            def _(y=y):
                add(y)


def rim_sums(order, n, arrived, turned, annot, sums):
    mine, chunks, _, _ = turned.shape
    samples = chunks * LANES
    return pl.pallas_call(
        functools.partial(rim_kernel, order),
        out_shape=(
            jax.ShapeDtypeStruct(sums.shape, jnp.float32),
            jax.ShapeDtypeStruct((sums.shape[0], TILE), jnp.float32),
        ),
        in_specs=[in_smem] + [in_vmem] * 4,
        out_specs=(in_vmem, in_vmem),
        scratch_shapes=[
            pltpu.VMEM((2, samples, LANES), jnp.bfloat16),
            pltpu.VMEM((samples, TILE), jnp.float32),
        ],
        compiler_params=pltpu.CompilerParams(vmem_limit_bytes=VMEM_LIMIT),
        cost_estimate=pl.CostEstimate(
            flops=2 * samples * TILE * mine * TILE,
            bytes_accessed=2 * samples * TILE * (mine + 1),
            transcendentals=0,
        ),
        name="rim_sums",
    )(n, arrived, turned, annot, sums)


def eye(size):
    shape = (size, size)
    return lax.broadcasted_iota(jnp.int32, shape, 0) == lax.broadcasted_iota(jnp.int32, shape, 1)


def upright(row):
    size = row.shape[1]
    return jnp.sum(jnp.where(eye(size), jnp.broadcast_to(row, (size, size)), 0.0), axis=1, keepdims=True)


def lying(column):
    size = column.shape[0]
    return jnp.sum(
        jnp.where(eye(size), jnp.broadcast_to(column, (size, size)), 0.0), axis=0, keepdims=True
    )


def moments_kernel(total_variants, n_ref, w_ref, counts_ref, sums_ref, first_ref, second_ref, scores_ref, payload_ref, whole):
    annots = counts_ref.shape[1]
    block = sums_ref.shape[1]
    mine = block // TILE
    n = n_ref[0]
    slot = 2 * w_ref[0] + n
    whole[...] = sums_ref[...]
    for order, back_ref in enumerate((first_ref, second_ref)):
        whole[:, cols_at((1 - n) * order + n * (mine - 1 - order))] += back_ref[...]
    shares = upright(counts_ref[...]) / total_variants
    high = (1.0 - shares).astype(jnp.bfloat16).astype(jnp.float32)
    low = (0.0 - shares).astype(jnp.bfloat16).astype(jnp.float32)
    members = whole[:annots, :]
    scores = high * members + low * (whole[annots : annots + 1, :] - members)
    scores_ref[:annots, :] = scores
    row = lax.broadcasted_iota(jnp.int32, (2 * PAD, block), 0)
    scores_ref[annots:, :] = jnp.where(row == 0, 1.0, 0.0)
    mean = jnp.sum(scores, axis=1, keepdims=True) / block
    deviation = scores - mean
    payload_ref[:annots, :] = lax.dot_general(
        deviation,
        deviation,
        (((1,), (1,)), ((), ())),
        precision=highest_precision,
        preferred_element_type=jnp.float32,
    )
    slots = payload_ref.shape[0] - annots
    at = lax.broadcasted_iota(jnp.int32, (slots, annots), 0)
    payload_ref[annots:, :] = jnp.where(at == slot, lying(mean), 0.0)


def moments_of(total_variants, slots, n, w, counts, sums, back):
    annots = counts.shape[1]
    block = sums.shape[1]
    return pl.pallas_call(
        functools.partial(moments_kernel, total_variants),
        out_shape=(
            jax.ShapeDtypeStruct((annots + 2 * PAD, block), jnp.float32),
            jax.ShapeDtypeStruct((annots + slots, annots), jnp.float32),
        ),
        in_specs=[in_smem] * 2 + [in_vmem] * 4,
        out_specs=(in_vmem, in_vmem),
        scratch_shapes=[pltpu.VMEM(sums.shape, jnp.float32)],
        compiler_params=pltpu.CompilerParams(vmem_limit_bytes=VMEM_LIMIT),
        cost_estimate=pl.CostEstimate(
            flops=12 * annots * annots * block, bytes_accessed=12 * annots * block, transcendentals=0
        ),
        name="moments",
    )(n, w, counts, sums, *back)


def inverse_kernel(divisor, payload_ref, inverse_ref, moments_ref):
    size = payload_ref.shape[1]
    slots = payload_ref.shape[0] - size
    means = payload_ref[size:, :]
    mean = jnp.sum(means, axis=0, keepdims=True) / slots
    between = means - mean
    covariance = (
        payload_ref[:size, :]
        + lax.dot_general(
            between,
            between,
            (((0,), (0,)), ((), ())),
            precision=highest_precision,
            preferred_element_type=jnp.float32,
        )
        * (divisor // slots)
    ) / divisor
    row = lax.broadcasted_iota(jnp.int32, (size, size), 0)
    lane = lax.broadcasted_iota(jnp.int32, (size, size), 1)
    diagonal = jnp.where(row == lane, covariance, 0.0)
    across = 1.0 / jnp.sqrt(jnp.sum(diagonal, axis=0, keepdims=True) + EPS)
    down = 1.0 / jnp.sqrt(jnp.sum(diagonal, axis=1, keepdims=True) + EPS)
    mean_down = jnp.sum(jnp.where(row == lane, jnp.broadcast_to(mean, (size, size)), 0.0), axis=1, keepdims=True)
    moments_ref[...] = jnp.where(lane == 0, mean_down, down)
    gram = covariance * down * across
    groups = [gram[PAD * g : PAD * (g + 1), :] for g in range(size // PAD)]
    lane_of = lax.broadcasted_iota(jnp.int32, (1, size), 1)
    row_of = lax.broadcasted_iota(jnp.int32, (PAD, size), 0)

    def pair_inverse(a, b, c):
        scale = 1.0 / (a * c - b * b)
        return c * scale, -b * scale, a * scale

    for k in range(0, size, PIVOTS):
        g, i = divmod(k, PAD)
        spread = [
            [jnp.broadcast_to(old[:, k + j : k + j + 1], (PAD, size)) for j in range(PIVOTS)]
            for old in groups
        ]
        m = [[spread[g][c][i + r : i + r + 1, :] for c in range(PIVOTS)] for r in range(PIVOTS)]
        rows = [
            groups[g][i + j : i + j + 1, :] - jnp.where(lane_of == k + j, 1.0, 0.0)
            for j in range(PIVOTS)
        ]
        a, b, c = pair_inverse(m[0][0], m[0][1], m[1][1])
        u = a * rows[0] + b * rows[1], b * rows[0] + c * rows[1]
        v = [(a * m[0][j] + b * m[1][j], b * m[0][j] + c * m[1][j]) for j in (2, 3)]
        rest = [rows[j] - m[0][j] * u[0] - m[1][j] * u[1] for j in (2, 3)]
        d, e, f = pair_inverse(
            m[2][2] - m[0][2] * v[0][0] - m[1][2] * v[0][1],
            m[2][3] - m[0][2] * v[1][0] - m[1][2] * v[1][1],
            m[3][3] - m[0][3] * v[1][0] - m[1][3] * v[1][1],
        )
        third = d * rest[0] + e * rest[1]
        fourth = e * rest[0] + f * rest[1]
        solved = [
            u[0] - v[0][0] * third - v[1][0] * fourth,
            u[1] - v[0][1] * third - v[1][1] * fourth,
            third,
            fourth,
        ]
        solved = [jnp.broadcast_to(value, (PAD, size)) for value in solved]
        for h, old in enumerate(groups):
            for j in range(PIVOTS):
                old = old - spread[h][j] * solved[j]
                if h == g:
                    old = old + jnp.where(row_of == i + j, solved[j], 0.0)
            groups[h] = old
    swept = jnp.concatenate(groups, axis=0)
    inverse = jnp.where(row == lane, 2.0, 0.0) - swept
    inverse_ref[...] = inverse * down * across / divisor


def gram_inverse(divisor, payload):
    size = payload.shape[1]
    square = jax.ShapeDtypeStruct((size, size), jnp.float32)
    return pl.pallas_call(
        functools.partial(inverse_kernel, divisor),
        out_shape=(square, square),
        in_specs=[in_vmem],
        out_specs=(in_vmem, in_vmem),
        compiler_params=pltpu.CompilerParams(vmem_limit_bytes=VMEM_LIMIT),
        cost_estimate=pl.CostEstimate(flops=20_000_000_000, bytes_accessed=4 * size * size, transcendentals=0),
        name="gram_inverse",
    )(payload)


def halves(value):
    upper = value.astype(jnp.bfloat16)
    return upper, (value - upper.astype(jnp.float32)).astype(jnp.bfloat16)


def fit_kernel(
    divisor, n_ref, inverse_ref, moments_ref, proj_ref, scores_ref, other_ref, own_ref, fitted_ref,
    own, fitted, went,
):
    annots, block = own.shape
    n = n_ref[0]
    mean = moments_ref[:, 0:1]
    centred = scores_ref[:annots, :] - mean
    own[...] = centred * moments_ref[:, 1:2]
    copies = [pltpu.make_async_copy(own, own_ref, went.at[0])]
    copies[0].start()
    sums = proj_ref[annots : annots + 1, :]
    coefficient = jnp.dot(
        inverse_ref[...],
        proj_ref[:annots, :] - mean * sums,
        precision=highest_precision,
        preferred_element_type=jnp.float32,
    )
    upper, lower = halves(coefficient)
    right = jnp.concatenate([upper, upper, lower], axis=0)
    for half, values in enumerate((centred, other_ref[...] - mean)):
        upper, lower = halves(values)
        left = jnp.concatenate([upper, lower, upper], axis=0)
        place = (1 - half) * n + half * (1 - n)
        for c in range(block // TILE):
            rows = pl.ds(half * block + c * TILE, TILE)
            fitted[rows, :] = sums / divisor + lax.dot_general(
                left[:, c * TILE : (c + 1) * TILE],
                right,
                (((0,), (0,)), ((), ())),
                preferred_element_type=jnp.float32,
            )
            target = pl.ds(pl.multiple_of(place * block + c * TILE, TILE), TILE)
            copies.append(
                pltpu.make_async_copy(
                    fitted.at[rows, :], fitted_ref.at[target, :], went.at[len(copies)]
                )
            )
            copies[-1].start()
    for copy in copies:
        copy.wait()


def fitted_values(divisor, n, inverse, moments, projection, scores, scores_other):
    annots, block = scores_other.shape
    traits = projection.shape[1]
    return pl.pallas_call(
        functools.partial(fit_kernel, divisor),
        out_shape=(
            jax.ShapeDtypeStruct((annots, block), jnp.float32),
            jax.ShapeDtypeStruct((2 * block, traits), jnp.float32),
        ),
        in_specs=[in_smem] + [in_vmem] * 5,
        out_specs=(in_place, in_place),
        scratch_shapes=[
            pltpu.VMEM((annots, block), jnp.float32),
            pltpu.VMEM((2 * block, traits), jnp.float32),
            pltpu.SemaphoreType.DMA((1 + 2 * (block // TILE),)),
        ],
        compiler_params=pltpu.CompilerParams(vmem_limit_bytes=VMEM_LIMIT),
        cost_estimate=pl.CostEstimate(
            flops=4 * annots * block * traits, bytes_accessed=8 * block * traits, transcendentals=0
        ),
        name="fitted_values",
    )(n, inverse, moments, projection, scores, scores_other)


def flipped(value, axis, bit):
    length = lax.axis_size(axis)
    return lax.ppermute(value, axis, [(i, i ^ bit) for i in range(length)])


def wide_bits():
    length = lax.axis_size("wide")
    bits = []
    bit = 1
    while bit < length:
        bits.append(bit)
        bit *= 2
    return bits


def added_kernel(first_ref, second_ref, out_ref):
    out_ref[...] = first_ref[...] + second_ref[...]


def added(first, second):
    return pl.pallas_call(
        added_kernel,
        out_shape=jax.ShapeDtypeStruct(first.shape, first.dtype),
        in_specs=[in_vmem, in_vmem],
        out_specs=in_vmem,
        compiler_params=pltpu.CompilerParams(vmem_limit_bytes=VMEM_LIMIT // 4),
        name="added",
    )(first, second)


def wide_sum(value):
    bits = wide_bits()
    for bit in bits[:1] + bits[2:] + bits[1:2]:
        value = added(value, flipped(value, "wide", bit))
    return value


def split(value):
    half = value.shape[0] // 2
    low = lax.axis_index("wide") % 2
    kept = lax.dynamic_slice_in_dim(value, low * half, half, 0)
    given = lax.dynamic_slice_in_dim(value, (1 - low) * half, half, 0)
    return kept + flipped(given, "wide", 1)


def long_sum(value):
    for bit in wide_bits()[1:]:
        value = value + flipped(value, "wide", bit)
    return value


def joined(kept):
    low = lax.axis_index("wide") % 2
    other = flipped(kept, "wide", 1)
    return jnp.where(low == 0, jnp.concatenate([kept, other], 0), jnp.concatenate([other, kept], 0))


def whole_step(dosage, annotations, test_statistic_table):
    _, strip = dosage.shape
    annots = annotations.shape[0]
    wide = lax.axis_size("wide")
    total_variants = wide * strip
    w = lax.axis_index("wide")
    n = lax.axis_index("narrow")
    block = strip // 2
    n_array = jnp.reshape(n, (1,)).astype(jnp.int32)

    rim_pairs = []
    back_pairs = []
    for i in range(wide - 1):
        rim_pairs += [(2 * i, 2 * i + 2), (2 * i + 3, 2 * i + 1)]
        back_pairs += [(2 * i + 1, 2 * i + 2), (2 * i + 2, 2 * i + 1)]
    chi = test_statistic_table
    arrived = []
    for outgoing in outgoing_columns(n_array, dosage, annotations):
        arrived.append(lax.ppermute(outgoing, both, rim_pairs))
    annot, counts, chi_given = prepared(n_array, annotations, chi)
    chi_other = flipped(chi_given, "narrow", 1)
    counts = wide_sum(counts)
    sums, turned = own_sums(n_array, dosage, annot)
    tiles = block // TILE
    pieces = tuple(range(tiles // 2)), tuple(range(tiles // 2, tiles))
    back = []
    for order in range(2):
        sums, part = rim_sums(order, n_array, arrived[order], turned, annot, sums)
        back.append(lax.ppermute(part, both, back_pairs))
        sums = other_sums(pieces[order], n_array, dosage, annot, turned, sums)

    w_array = jnp.reshape(w, (1,)).astype(jnp.int32)
    extended, payload = moments_of(total_variants, 2 * wide, n_array, w_array, counts, sums, back)
    scores = extended[:annots]
    payload = split(payload)
    payload = payload + flipped(payload, "narrow", 1)
    payload = joined(long_sum(payload))

    chi_own = lax.dynamic_slice_in_dim(chi, n * block, block, 0)
    halves_of = [
        jnp.dot(extended, values, precision=lax.Precision.HIGH, preferred_element_type=jnp.float32)
        for values in (chi_other, chi_own)
    ]
    projection = split(jnp.concatenate(halves_of, axis=1))
    traits = chi.shape[1]
    projection = projection[:, traits:] + flipped(projection[:, :traits], "narrow", 1)
    projection = joined(long_sum(projection))
    scores_other = flipped(scores, "narrow", 1)

    inverse, moments = gram_inverse(total_variants, payload)
    return fitted_values(
        total_variants, n_array, inverse, moments, projection, extended, scores_other
    )


def solution(mesh):
    in_specs = (P(None, "wide"), P(None, "wide"), P("wide", "narrow"))
    out_specs = (P(None, both), P("wide", "narrow"))
    return jax.shard_map(whole_step, mesh=mesh, in_specs=in_specs, out_specs=out_specs, check_vma=False)
```

profile of v0, /device:TPU:0, one launch (start us, length us, event | category | flops | bytes accessed | tf_op | source)
XLA Modules:
  0.0 111.7 jit_solution(7753311528940308915)
XLA Ops:
  0.6 3.2 %outgoing.1 = (bf16[2184,256]{1,0:T(8,128)(2,1)}, bf16[2184,256]{1,0:T(8,128)(2,1)}) custom-call(s32[1]{0:T(128)} %bitcast.n_ref, bf16[2048,2048]{1,0:T(8,128)(2,1)} %dosage_ref.7, s32[128,2048]{1,0:T(8,128)} %annot_ref.3), custom_call_target="tpu_custom_call" | custom-call | bytes 4194304 | tf_op jit(solution)/shard_map/outgoing/pallas_call | solution.py:132
  3.9 3.4 %collective-permute-start.5 = (bf16[2184,256]{1,0:T(8,128)(2,1)}, bf16[2184,256]{1,0:T(8,128)(2,1)}, u32[]{:S(2)}, u32[]{:S(2)}) collective-permute-start(bf16[2184,256]{1,0:T(8,128)(2,1)} %get-tuple-element.21), channel_id=1, source_target_pairs={{0,2},{3,1},{2,4},{5,3},{4,6},{7,5},{6,8},{9,7},{8,10},{11,9},{10,... | collective-permute-start | bytes 3354632 | tf_op jit(solution)/shard_map/ppermute | solution.py:650
  7.3 4.5 %collective-permute-start.4 = (bf16[2184,256]{1,0:T(8,128)(2,1)}, bf16[2184,256]{1,0:T(8,128)(2,1)}, u32[]{:S(2)}, u32[]{:S(2)}) collective-permute-start(bf16[2184,256]{1,0:T(8,128)(2,1)} %get-tuple-element.20), channel_id=1, source_target_pairs={{0,2},{3,1},{2,4},{5,3},{4,6},{7,5},{6,8},{9,7},{8,10},{11,9},{10,... | collective-permute-start | bytes 3354632 | tf_op jit(solution)/shard_map/ppermute | solution.py:650
  11.8 1.2 %copy-done.7 = s32[128,2048]{1,0:T(8,128)S(1)} copy-done((s32[128,2048]{1,0:T(8,128)S(1)}, s32[128,2048]{1,0:T(8,128)}, u32[]{:S(2)}) %copy-start.7) | copy-done | bytes 1048600
  13.0 1.3 %prepare.1 = (bf16[136,2048]{1,0:T(8,128)(2,1)S(1)}, f32[1,128]{1,0:T(1,128)S(1)}, f32[1024,256]{1,0:T(8,128)}) custom-call(s32[1]{0:T(128)} %bitcast.n_ref, s32[128,2048]{1,0:T(8,128)S(1)} %copy-done.7, f32[2048,256]{1,0:T(8,128)S(1)} %copy-done.6), custom_call_target="tpu_custom_call" | custom-call | bytes 4194304 | tf_op jit(solution)/shard_map/prepare/pallas_call | solution.py:162
  14.3 0.1 collective-permute-start
  14.4 0.1 collective-permute-start.14
  14.5 3.4 %copy-done.3 = bf16[2048,2048]{1,0:T(8,128)(2,1)S(1)} copy-done((bf16[2048,2048]{1,0:T(8,128)(2,1)S(1)}, bf16[2048,2048]{1,0:T(8,128)(2,1)}, u32[]{:S(2)}) %copy-start.3) | copy-done | bytes 8388632
  17.9 7.2 %own_sums.1 = (f32[136,1024]{1,0:T(8,128)S(1)}, bf16[4,16,256,128]{3,2,1,0:T(8,128)(2,1)S(1)}) custom-call(s32[1]{0:T(128)} %bitcast.n_ref, bf16[2048,2048]{1,0:T(8,128)(2,1)S(1)} %copy-done.3, bf16[136,2048]{1,0:T(8,128)(2,1)S(1)} %get-tuple-element.18.annot_ref), custom_call_target="tpu_custom_call" | custom-call | flops 4294967296 | bytes 8388608 | tf_op jit(solution)/shard_map/own_sums/pallas_call | solution.py:252
  25.1 2.0 %copy-done = bf16[4,16,256,128]{3,2,1,0:T(8,128)(2,1)} copy-done((bf16[4,16,256,128]{3,2,1,0:T(8,128)(2,1)}, bf16[4,16,256,128]{3,2,1,0:T(8,128)(2,1)S(1)}, u32[]{:S(2)}) %copy-start) | copy-done | bytes 4194328
  27.0 2.0 %collective-permute-start.1 = (f32[1,128]{1,0:T(1,128)S(1)}, f32[1,128]{1,0:T(1,128)S(1)}, u32[]{:S(2)}, u32[]{:S(2)}) collective-permute-start(f32[1,128]{1,0:T(1,128)S(1)} %added.4.first_ref), channel_id=1, source_target_pairs={{0,8},{2,10},{4,12},{6,14},{8,0},{10,2},{12,4},{14,6},{16,24},{18,... | collective-permute-start | bytes 1544 | tf_op jit(solution)/shard_map/ppermute | solution.py:577
  29.0 1.6 %collective-permute-done.1.second_ref = f32[1,128]{1,0:T(1,128)S(1)} collective-permute-done((f32[1,128]{1,0:T(1,128)S(1)}, f32[1,128]{1,0:T(1,128)S(1)}, u32[]{:S(2)}, u32[]{:S(2)}) %collective-permute-start.1) | collective-permute-done | bytes 544 | tf_op jit(solution)/shard_map/ppermute | solution.py:577
  30.6 3.0 %collective-permute-start.2 = (f32[1,128]{1,0:T(1,128)S(1)}, f32[1,128]{1,0:T(1,128)S(1)}, u32[]{:S(2)}, u32[]{:S(2)}) collective-permute-start(f32[1,128]{1,0:T(1,128)S(1)} %added.5.first_ref), channel_id=1, source_target_pairs={{0,16},{2,18},{4,20},{6,22},{8,24},{10,26},{12,28},{14,30},{16,0},... | collective-permute-start | bytes 1544 | tf_op jit(solution)/shard_map/ppermute | solution.py:577
  33.6 1.5 %collective-permute-done.2.second_ref = f32[1,128]{1,0:T(1,128)S(1)} collective-permute-done((f32[1,128]{1,0:T(1,128)S(1)}, f32[1,128]{1,0:T(1,128)S(1)}, u32[]{:S(2)}, u32[]{:S(2)}) %collective-permute-start.2) | collective-permute-done | bytes 544 | tf_op jit(solution)/shard_map/ppermute | solution.py:577
  35.1 1.4 %collective-permute-start.3 = (f32[1,128]{1,0:T(1,128)S(1)}, f32[1,128]{1,0:T(1,128)S(1)}, u32[]{:S(2)}, u32[]{:S(2)}) collective-permute-start(f32[1,128]{1,0:T(1,128)S(1)} %added.6.first_ref), channel_id=1, source_target_pairs={{0,4},{2,6},{4,0},{6,2},{8,12},{10,14},{12,8},{14,10},{16,20},{18,... | collective-permute-start | bytes 1544 | tf_op jit(solution)/shard_map/ppermute | solution.py:577
  36.5 2.2 %collective-permute-done.3.second_ref = f32[1,128]{1,0:T(1,128)S(1)} collective-permute-done((f32[1,128]{1,0:T(1,128)S(1)}, f32[1,128]{1,0:T(1,128)S(1)}, u32[]{:S(2)}, u32[]{:S(2)}) %collective-permute-start.3) | collective-permute-done | bytes 544 | tf_op jit(solution)/shard_map/ppermute | solution.py:577
  38.7 2.2 %copy-done.1 = bf16[4,16,256,128]{3,2,1,0:T(8,128)(2,1)S(1)} copy-done((bf16[4,16,256,128]{3,2,1,0:T(8,128)(2,1)S(1)}, bf16[4,16,256,128]{3,2,1,0:T(8,128)(2,1)}, u32[]{:S(2)}) %copy-start.1) | copy-done | bytes 4194328
  40.9 5.1 %rim_sums.2 = (f32[136,1024]{1,0:T(8,128)S(1)}, f32[136,256]{1,0:T(8,128)S(1)}) custom-call(s32[1]{0:T(128)} %bitcast.n_ref, bf16[2184,256]{1,0:T(8,128)(2,1)} %collective-permute-done.5.arrived_ref, bf16[4,16,256,128]{3,2,1,0:T(8,128)(2,1)S(1)} %copy-done.1, bf16[136,2048]{1,0:T(8,128)(2,1)S(1)} %get-tuple-element.18.annot_ref, ...), custom_call_target="tpu_custom_call" | custom-call | flops 1073741824 | bytes 5242880 | tf_op jit(solution)/shard_map/rim_sums/pallas_call | solution.py:326
  46.0 3.4 %copy-done.4 = bf16[2048,2048]{1,0:T(8,128)(2,1)S(1)} copy-done((bf16[2048,2048]{1,0:T(8,128)(2,1)S(1)}, bf16[2048,2048]{1,0:T(8,128)(2,1)}, u32[]{:S(2)}) %copy-start.4) | copy-done | bytes 8388632
  49.3 5.6 %other_sums.2.sums_in = f32[136,1024]{1,0:T(8,128)S(1)} custom-call(s32[1]{0:T(128)} %bitcast.n_ref, bf16[2048,2048]{1,0:T(8,128)(2,1)S(1)} %copy-done.4, bf16[136,2048]{1,0:T(8,128)(2,1)S(1)} %get-tuple-element.18.annot_ref, bf16[4,16,256,128]{3,2,1,0:T(8,128)(2,1)S(1)} %copy-done.2, f32[136,1024]{1,0:T(8,128)S(1)} %get-tuple-element.23.sums_in), custom_call_target="tpu_custom_call" | custom-call | flops 4294967296 | bytes 8388608 | tf_op jit(solution)/shard_map/other_sums/pallas_call | solution.py:268
  55.0 2.5 %rim_sums.3 = (f32[136,1024]{1,0:T(8,128)S(1)}, f32[136,256]{1,0:T(8,128)S(1)}) custom-call(s32[1]{0:T(128)} %bitcast.n_ref, bf16[2184,256]{1,0:T(8,128)(2,1)} %collective-permute-done.4.arrived_ref, bf16[4,16,256,128]{3,2,1,0:T(8,128)(2,1)S(1)} %copy-done.2, bf16[136,2048]{1,0:T(8,128)(2,1)S(1)} %get-tuple-element.18.annot_ref, ...), custom_call_target="tpu_custom_call" | custom-call | flops 1073741824 | bytes 5242880 | tf_op jit(solution)/shard_map/rim_sums/pallas_call | solution.py:326
  57.4 0.7 collective-permute-start.7
  58.1 0.9 collective-permute-start.6
  59.0 2.8 %other_sums.3.sums_ref = f32[136,1024]{1,0:T(8,128)S(1)} custom-call(s32[1]{0:T(128)} %bitcast.n_ref, bf16[2048,2048]{1,0:T(8,128)(2,1)S(1)} %copy-done.5, bf16[136,2048]{1,0:T(8,128)(2,1)S(1)} %get-tuple-element.18.annot_ref, bf16[4,16,256,128]{3,2,1,0:T(8,128)(2,1)S(1)} %copy-done.2, f32[136,1024]{1,0:T(8,128)S(1)} %get-tuple-element.24.sums_in), custom_call_target="tpu_custom_call" | custom-call | flops 4294967296 | bytes 8388608 | tf_op jit(solution)/shard_map/other_sums/pallas_call | solution.py:268
  61.8 0.9 moments.1
  62.7 0.4 fusion
  63.2 1.7 %fusion.6 = f32[144,256]{1,0:T(8,128)S(1)} fusion(f32[144,1024]{1,0:T(8,128)S(1)} %get-tuple-element.30.scores_ref, f32[1024,256]{1,0:T(8,128)} %collective-permute-done.14), kind=kOutput, calls=%fused_computation.15 | convolution fusion | flops 226492416 | bytes 1785856 | tf_op jit(solution)/shard_map/dot_general | solution.py:672
  64.9 10.3 %collective-permute-start.15 = (f32[72,512]{1,0:T(8,128)S(1)}, f32[72,512]{1,0:T(8,128)S(1)}, u32[]{:S(2)}, u32[]{:S(2)}) collective-permute-start(f32[72,512]{1,0:T(8,128)S(1)} %fusion.2), channel_id=1, source_target_pairs={{0,2},{2,0},{4,6},{6,4},{8,10},{10,8},{12,14},{14,12},{16,18},{18,... | collective-permute-start | bytes 442376 | tf_op jit(solution)/shard_map/ppermute | solution.py:577
  75.1 0.1 collective-permute-start.8
  75.3 0.9 collective-permute-done.15
  76.2 1.1 collective-permute-start.16
  77.3 1.1 collective-permute-start.9
  78.4 3.3 %collective-permute-done.9 = f32[80,128]{1,0:T(8,128)S(1)} collective-permute-done((f32[80,128]{1,0:T(8,128)S(1)}, f32[80,128]{1,0:T(8,128)S(1)}, u32[]{:S(2)}, u32[]{:S(2)}) %collective-permute-start.9) | collective-permute-done | bytes 40992 | tf_op jit(solution)/shard_map/ppermute | solution.py:577
  81.7 0.4 collective-permute-start.10
  82.1 1.7 %collective-permute-start.17 = (f32[72,256]{1,0:T(8,128)S(1)}, f32[72,256]{1,0:T(8,128)S(1)}, u32[]{:S(2)}, u32[]{:S(2)}) collective-permute-start(f32[72,256]{1,0:T(8,128)S(1)} %slice_add_fusion), channel_id=1, source_target_pairs={{0,4},{2,6},{4,0},{6,2},{8,12},{10,14},{12,8},{14,10},{16,20},{18,... | collective-permute-start | bytes 221192 | tf_op jit(solution)/shard_map/ppermute | solution.py:577
  83.8 1.9 %collective-permute-done.10 = f32[80,128]{1,0:T(8,128)S(1)} collective-permute-done((f32[80,128]{1,0:T(8,128)S(1)}, f32[80,128]{1,0:T(8,128)S(1)}, u32[]{:S(2)}, u32[]{:S(2)}) %collective-permute-start.10) | collective-permute-done | bytes 40992 | tf_op jit(solution)/shard_map/ppermute | solution.py:577
  85.7 0.1 collective-permute-start.11
  85.7 3.9 %collective-permute-done.11 = f32[80,128]{1,0:T(8,128)S(1)} collective-permute-done((f32[80,128]{1,0:T(8,128)S(1)}, f32[80,128]{1,0:T(8,128)S(1)}, u32[]{:S(2)}, u32[]{:S(2)}) %collective-permute-start.11) | collective-permute-done | bytes 40992 | tf_op jit(solution)/shard_map/ppermute | solution.py:577
  89.7 2.6 %collective-permute-start.12 = (f32[80,128]{1,0:T(8,128)S(1)}, f32[80,128]{1,0:T(8,128)S(1)}, u32[]{:S(2)}, u32[]{:S(2)}) collective-permute-start(f32[80,128]{1,0:T(8,128)S(1)} %add.58), channel_id=1, source_target_pairs={{0,16},{2,18},{4,20},{6,22},{8,24},{10,26},{12,28},{14,30},{16,0},... | collective-permute-start | bytes 122888 | tf_op jit(solution)/shard_map/ppermute | solution.py:577
  92.3 0.1 collective-permute-start.18
  92.4 2.2 %collective-permute-done.12 = f32[80,128]{1,0:T(8,128)S(1)} collective-permute-done((f32[80,128]{1,0:T(8,128)S(1)}, f32[80,128]{1,0:T(8,128)S(1)}, u32[]{:S(2)}, u32[]{:S(2)}) %collective-permute-start.12) | collective-permute-done | bytes 40992 | tf_op jit(solution)/shard_map/ppermute | solution.py:577
  94.7 1.1 %collective-permute-start.21 = (f32[128,1024]{1,0:T(8,128)S(1)}, f32[128,1024]{1,0:T(8,128)S(1)}, u32[]{:S(2)}, u32[]{:S(2)}) collective-permute-start(f32[128,1024]{1,0:T(8,128)S(1)} %slice.11), channel_id=1, source_target_pairs={{0,1},{1,0},{2,3},{3,2},{4,5},{5,4},{6,7},{7,6},{8,9},{9,8},{10,11... | collective-permute-start | bytes 1572872 | tf_op jit(solution)/shard_map/ppermute | solution.py:577
  95.8 1.0 collective-permute-done.18
  96.8 2.0 %collective-permute-start.19 = (f32[72,256]{1,0:T(8,128)S(1)}, f32[72,256]{1,0:T(8,128)S(1)}, u32[]{:S(2)}, u32[]{:S(2)}) collective-permute-start(f32[72,256]{1,0:T(8,128)S(1)} %add.66), channel_id=1, source_target_pairs={{0,16},{2,18},{4,20},{6,22},{8,24},{10,26},{12,28},{14,30},{16,0},... | collective-permute-start | bytes 221192 | tf_op jit(solution)/shard_map/ppermute | solution.py:577
  98.8 3.9 %collective-permute-done.19 = f32[72,256]{1,0:T(8,128)S(1)} collective-permute-done((f32[72,256]{1,0:T(8,128)S(1)}, f32[72,256]{1,0:T(8,128)S(1)}, u32[]{:S(2)}, u32[]{:S(2)}) %collective-permute-start.19) | collective-permute-done | bytes 73760 | tf_op jit(solution)/shard_map/ppermute | solution.py:577
  102.7 0.1 collective-permute-start.20
  102.8 6.5 %gram_inverse.1 = (f32[128,128]{1,0:T(8,128)S(1)}, f32[128,128]{1,0:T(8,128)S(1)}) custom-call(f32[160,128]{1,0:T(8,128)S(1)} %maximum_select_fusion.1.payload_ref), custom_call_target="tpu_custom_call" | custom-call | flops 20000000000 | bytes 65536 | tf_op jit(solution)/shard_map/gram_inverse/pallas_call | solution.py:492
  109.4 2.1 %fitted_values.1 = (f32[128,1024]{1,0:T(8,128)}, f32[2048,256]{1,0:T(8,128)}) custom-call(s32[1]{0:T(128)} %bitcast.n_ref, f32[128,128]{1,0:T(8,128)S(1)} %get-tuple-element.28.inverse_ref, f32[128,128]{1,0:T(8,128)S(1)} %get-tuple-element.29.moments_ref, f32[144,256]{1,0:T(8,128)S(1)} %maximum_select_fusion.proj_ref, ...), custom_call_target="tpu_custom_call" | custom-call | flops 134217728 | bytes 2097152 | tf_op jit(solution)/shard_map/fitted_values/pallas_call | solution.py:554
  (44 shorter events, 0.3 us)
Async XLA Ops:
  0.6 11.2 %copy-start.6 = (f32[2048,256]{1,0:T(8,128)S(1)}, f32[2048,256]{1,0:T(8,128)}, u32[]{:S(2)}) copy-start(f32[2048,256]{1,0:T(8,128)} %chi_ref.1) | copy-start | bytes 6291460
  3.9 34.8 %collective-permute-start.5 = (bf16[2184,256]{1,0:T(8,128)(2,1)}, bf16[2184,256]{1,0:T(8,128)(2,1)}, u32[]{:S(2)}, u32[]{:S(2)}) collective-permute-start(bf16[2184,256]{1,0:T(8,128)(2,1)} %get-tuple-element.21), channel_id=1, source_target_pairs={{0,2},{3,1},{2,4},{5,3},{4,6},{7,5},{6,8},{9,7},{8,10},{11,9},{10,... | collective-permute-start | bytes 3354632 | tf_op jit(solution)/shard_map/ppermute | solution.py:650
  7.3 47.7 %collective-permute-start.4 = (bf16[2184,256]{1,0:T(8,128)(2,1)}, bf16[2184,256]{1,0:T(8,128)(2,1)}, u32[]{:S(2)}, u32[]{:S(2)}) collective-permute-start(bf16[2184,256]{1,0:T(8,128)(2,1)} %get-tuple-element.20), channel_id=1, source_target_pairs={{0,2},{3,1},{2,4},{5,3},{4,6},{7,5},{6,8},{9,7},{8,10},{11,9},{10,... | collective-permute-start | bytes 3354632 | tf_op jit(solution)/shard_map/ppermute | solution.py:650
  11.8 1.2 %copy-start.7 = (s32[128,2048]{1,0:T(8,128)S(1)}, s32[128,2048]{1,0:T(8,128)}, u32[]{:S(2)}) copy-start(s32[128,2048]{1,0:T(8,128)} %annot_ref.3) | copy-start | bytes 3145732
  14.3 12.7 %collective-permute-start = (f32[1,128]{1,0:T(1,128)S(1)}, f32[1,128]{1,0:T(1,128)S(1)}, u32[]{:S(2)}, u32[]{:S(2)}) collective-permute-start(f32[1,128]{1,0:T(1,128)S(1)} %get-tuple-element.17.first_ref), channel_id=1, source_target_pairs={{0,2},{2,0},{4,6},{6,4},{8,10},{10,8},{12,14},{14,12},{16,18},{18,... | collective-permute-start | bytes 1544 | tf_op jit(solution)/shard_map/ppermute | solution.py:577
  14.4 48.8 %collective-permute-start.14 = (f32[1024,256]{1,0:T(8,128)}, f32[1024,256]{1,0:T(8,128)}, u32[]{:S(2)}, u32[]{:S(2)}) collective-permute-start(f32[1024,256]{1,0:T(8,128)} %get-tuple-element.31), channel_id=1, source_target_pairs={{0,1},{1,0},{2,3},{3,2},{4,5},{5,4},{6,7},{7,6},{8,9},{9,8},{10,11... | collective-permute-start | bytes 3145736 | tf_op jit(solution)/shard_map/ppermute | solution.py:577
  14.5 3.4 %copy-start.3 = (bf16[2048,2048]{1,0:T(8,128)(2,1)S(1)}, bf16[2048,2048]{1,0:T(8,128)(2,1)}, u32[]{:S(2)}) copy-start(bf16[2048,2048]{1,0:T(8,128)(2,1)} %dosage_ref.7) | copy-start | bytes 25165828
  25.1 2.0 %copy-start = (bf16[4,16,256,128]{3,2,1,0:T(8,128)(2,1)}, bf16[4,16,256,128]{3,2,1,0:T(8,128)(2,1)S(1)}, u32[]{:S(2)}) copy-start(bf16[4,16,256,128]{3,2,1,0:T(8,128)(2,1)S(1)} %get-tuple-element.19.turned_ref) | copy-start | bytes 12582916
  27.0 3.6 %collective-permute-start.1 = (f32[1,128]{1,0:T(1,128)S(1)}, f32[1,128]{1,0:T(1,128)S(1)}, u32[]{:S(2)}, u32[]{:S(2)}) collective-permute-start(f32[1,128]{1,0:T(1,128)S(1)} %added.4.first_ref), channel_id=1, source_target_pairs={{0,8},{2,10},{4,12},{6,14},{8,0},{10,2},{12,4},{14,6},{16,24},{18,... | collective-permute-start | bytes 1544 | tf_op jit(solution)/shard_map/ppermute | solution.py:577
  30.6 4.5 %collective-permute-start.2 = (f32[1,128]{1,0:T(1,128)S(1)}, f32[1,128]{1,0:T(1,128)S(1)}, u32[]{:S(2)}, u32[]{:S(2)}) collective-permute-start(f32[1,128]{1,0:T(1,128)S(1)} %added.5.first_ref), channel_id=1, source_target_pairs={{0,16},{2,18},{4,20},{6,22},{8,24},{10,26},{12,28},{14,30},{16,0},... | collective-permute-start | bytes 1544 | tf_op jit(solution)/shard_map/ppermute | solution.py:577
  35.1 3.6 %collective-permute-start.3 = (f32[1,128]{1,0:T(1,128)S(1)}, f32[1,128]{1,0:T(1,128)S(1)}, u32[]{:S(2)}, u32[]{:S(2)}) collective-permute-start(f32[1,128]{1,0:T(1,128)S(1)} %added.6.first_ref), channel_id=1, source_target_pairs={{0,4},{2,6},{4,0},{6,2},{8,12},{10,14},{12,8},{14,10},{16,20},{18,... | collective-permute-start | bytes 1544 | tf_op jit(solution)/shard_map/ppermute | solution.py:577
  38.7 2.2 %copy-start.1 = (bf16[4,16,256,128]{3,2,1,0:T(8,128)(2,1)S(1)}, bf16[4,16,256,128]{3,2,1,0:T(8,128)(2,1)}, u32[]{:S(2)}) copy-start(bf16[4,16,256,128]{3,2,1,0:T(8,128)(2,1)} %copy-done) | copy-start | bytes 12582916
  40.9 5.1 %copy-start.2 = (bf16[4,16,256,128]{3,2,1,0:T(8,128)(2,1)S(1)}, bf16[4,16,256,128]{3,2,1,0:T(8,128)(2,1)}, u32[]{:S(2)}) copy-start(bf16[4,16,256,128]{3,2,1,0:T(8,128)(2,1)} %copy-done) | copy-start | bytes 12582916
  46.0 3.4 %copy-start.4 = (bf16[2048,2048]{1,0:T(8,128)(2,1)S(1)}, bf16[2048,2048]{1,0:T(8,128)(2,1)}, u32[]{:S(2)}) copy-start(bf16[2048,2048]{1,0:T(8,128)(2,1)} %dosage_ref.7) | copy-start | bytes 25165828
  49.3 9.7 %copy-start.5 = (bf16[2048,2048]{1,0:T(8,128)(2,1)S(1)}, bf16[2048,2048]{1,0:T(8,128)(2,1)}, u32[]{:S(2)}) copy-start(bf16[2048,2048]{1,0:T(8,128)(2,1)} %dosage_ref.7) | copy-start | bytes 25165828
  57.4 4.4 %collective-permute-start.7 = (f32[136,256]{1,0:T(8,128)S(1)}, f32[136,256]{1,0:T(8,128)S(1)}, u32[]{:S(2)}, u32[]{:S(2)}) collective-permute-start(f32[136,256]{1,0:T(8,128)S(1)} %get-tuple-element.26), channel_id=1, source_target_pairs={{1,2},{2,1},{3,4},{4,3},{5,6},{6,5},{7,8},{8,7},{9,10},{10,9},{11,... | collective-permute-start | bytes 417800 | tf_op jit(solution)/shard_map/ppermute | solution.py:660
  58.1 3.7 %collective-permute-start.6 = (f32[136,256]{1,0:T(8,128)S(1)}, f32[136,256]{1,0:T(8,128)S(1)}, u32[]{:S(2)}, u32[]{:S(2)}) collective-permute-start(f32[136,256]{1,0:T(8,128)S(1)} %get-tuple-element.25), channel_id=1, source_target_pairs={{1,2},{2,1},{3,4},{4,3},{5,6},{6,5},{7,8},{8,7},{9,10},{10,9},{11,... | collective-permute-start | bytes 417800 | tf_op jit(solution)/shard_map/ppermute | solution.py:660
  64.9 11.3 %collective-permute-start.15 = (f32[72,512]{1,0:T(8,128)S(1)}, f32[72,512]{1,0:T(8,128)S(1)}, u32[]{:S(2)}, u32[]{:S(2)}) collective-permute-start(f32[72,512]{1,0:T(8,128)S(1)} %fusion.2), channel_id=1, source_target_pairs={{0,2},{2,0},{4,6},{6,4},{8,10},{10,8},{12,14},{14,12},{16,18},{18,... | collective-permute-start | bytes 442376 | tf_op jit(solution)/shard_map/ppermute | solution.py:577
  75.1 2.1 %collective-permute-start.8 = (f32[80,128]{1,0:T(8,128)S(1)}, f32[80,128]{1,0:T(8,128)S(1)}, u32[]{:S(2)}, u32[]{:S(2)}) collective-permute-start(f32[80,128]{1,0:T(8,128)S(1)} %constant_dynamic-slice_fusion), channel_id=1, source_target_pairs={{0,2},{2,0},{4,6},{6,4},{8,10},{10,8},{12,14},{14,12},{16,18},{18,... | collective-permute-start | bytes 122888 | tf_op jit(solution)/shard_map/ppermute | solution.py:577
  76.2 5.9 %collective-permute-start.16 = (f32[72,256]{1,0:T(8,128)S(1)}, f32[72,256]{1,0:T(8,128)S(1)}, u32[]{:S(2)}, u32[]{:S(2)}) collective-permute-start(f32[72,256]{1,0:T(8,128)S(1)} %slice.13), channel_id=1, source_target_pairs={{0,1},{1,0},{2,3},{3,2},{4,5},{5,4},{6,7},{7,6},{8,9},{9,8},{10,11... | collective-permute-start | bytes 221192 | tf_op jit(solution)/shard_map/ppermute | solution.py:577
  77.3 4.4 %collective-permute-start.9 = (f32[80,128]{1,0:T(8,128)S(1)}, f32[80,128]{1,0:T(8,128)S(1)}, u32[]{:S(2)}, u32[]{:S(2)}) collective-permute-start(f32[80,128]{1,0:T(8,128)S(1)} %dynamic-slice_add_fusion), channel_id=1, source_target_pairs={{0,1},{1,0},{2,3},{3,2},{4,5},{5,4},{6,7},{7,6},{8,9},{9,8},{10,11... | collective-permute-start | bytes 122888 | tf_op jit(solution)/shard_map/ppermute | solution.py:577
  81.7 4.0 %collective-permute-start.10 = (f32[80,128]{1,0:T(8,128)S(1)}, f32[80,128]{1,0:T(8,128)S(1)}, u32[]{:S(2)}, u32[]{:S(2)}) collective-permute-start(f32[80,128]{1,0:T(8,128)S(1)} %add.56), channel_id=1, source_target_pairs={{0,4},{2,6},{4,0},{6,2},{8,12},{10,14},{12,8},{14,10},{16,20},{18,... | collective-permute-start | bytes 122888 | tf_op jit(solution)/shard_map/ppermute | solution.py:577
  82.1 10.2 %collective-permute-start.17 = (f32[72,256]{1,0:T(8,128)S(1)}, f32[72,256]{1,0:T(8,128)S(1)}, u32[]{:S(2)}, u32[]{:S(2)}) collective-permute-start(f32[72,256]{1,0:T(8,128)S(1)} %slice_add_fusion), channel_id=1, source_target_pairs={{0,4},{2,6},{4,0},{6,2},{8,12},{10,14},{12,8},{14,10},{16,20},{18,... | collective-permute-start | bytes 221192 | tf_op jit(solution)/shard_map/ppermute | solution.py:577
  85.7 4.0 %collective-permute-start.11 = (f32[80,128]{1,0:T(8,128)S(1)}, f32[80,128]{1,0:T(8,128)S(1)}, u32[]{:S(2)}, u32[]{:S(2)}) collective-permute-start(f32[80,128]{1,0:T(8,128)S(1)} %add.57), channel_id=1, source_target_pairs={{0,8},{2,10},{4,12},{6,14},{8,0},{10,2},{12,4},{14,6},{16,24},{18,... | collective-permute-start | bytes 122888 | tf_op jit(solution)/shard_map/ppermute | solution.py:577
  89.7 4.9 %collective-permute-start.12 = (f32[80,128]{1,0:T(8,128)S(1)}, f32[80,128]{1,0:T(8,128)S(1)}, u32[]{:S(2)}, u32[]{:S(2)}) collective-permute-start(f32[80,128]{1,0:T(8,128)S(1)} %add.58), channel_id=1, source_target_pairs={{0,16},{2,18},{4,20},{6,22},{8,24},{10,26},{12,28},{14,30},{16,0},... | collective-permute-start | bytes 122888 | tf_op jit(solution)/shard_map/ppermute | solution.py:577
  92.3 4.4 %collective-permute-start.18 = (f32[72,256]{1,0:T(8,128)S(1)}, f32[72,256]{1,0:T(8,128)S(1)}, u32[]{:S(2)}, u32[]{:S(2)}) collective-permute-start(f32[72,256]{1,0:T(8,128)S(1)} %add.65), channel_id=1, source_target_pairs={{0,8},{2,10},{4,12},{6,14},{8,0},{10,2},{12,4},{14,6},{16,24},{18,... | collective-permute-start | bytes 221192 | tf_op jit(solution)/shard_map/ppermute | solution.py:577
  94.6 4.2 %collective-permute-start.13 = (f32[80,128]{1,0:T(8,128)S(1)}, f32[80,128]{1,0:T(8,128)S(1)}, u32[]{:S(2)}, u32[]{:S(2)}) collective-permute-start(f32[80,128]{1,0:T(8,128)S(1)} %add.59), channel_id=1, source_target_pairs={{0,2},{2,0},{4,6},{6,4},{8,10},{10,8},{12,14},{14,12},{16,18},{18,... | collective-permute-start | bytes 122888 | tf_op jit(solution)/shard_map/ppermute | solution.py:577
  94.7 14.7 %collective-permute-start.21 = (f32[128,1024]{1,0:T(8,128)S(1)}, f32[128,1024]{1,0:T(8,128)S(1)}, u32[]{:S(2)}, u32[]{:S(2)}) collective-permute-start(f32[128,1024]{1,0:T(8,128)S(1)} %slice.11), channel_id=1, source_target_pairs={{0,1},{1,0},{2,3},{3,2},{4,5},{5,4},{6,7},{7,6},{8,9},{9,8},{10,11... | collective-permute-start | bytes 1572872 | tf_op jit(solution)/shard_map/ppermute | solution.py:577
  96.8 5.9 %collective-permute-start.19 = (f32[72,256]{1,0:T(8,128)S(1)}, f32[72,256]{1,0:T(8,128)S(1)}, u32[]{:S(2)}, u32[]{:S(2)}) collective-permute-start(f32[72,256]{1,0:T(8,128)S(1)} %add.66), channel_id=1, source_target_pairs={{0,16},{2,18},{4,20},{6,22},{8,24},{10,26},{12,28},{14,30},{16,0},... | collective-permute-start | bytes 221192 | tf_op jit(solution)/shard_map/ppermute | solution.py:577
  102.7 6.6 %collective-permute-start.20 = (f32[72,256]{1,0:T(8,128)S(1)}, f32[72,256]{1,0:T(8,128)S(1)}, u32[]{:S(2)}, u32[]{:S(2)}) collective-permute-start(f32[72,256]{1,0:T(8,128)S(1)} %add.67), channel_id=1, source_target_pairs={{0,2},{2,0},{4,6},{6,4},{8,10},{10,8},{12,14},{14,12},{16,18},{18,... | collective-permute-start | bytes 221192 | tf_op jit(solution)/shard_map/ppermute | solution.py:577
where the time goes:
time: 112 us
  Pallas kernels  37.2 us (33%)
  starting transfers between devices  36.5 us (33%)
  waiting for transfers between devices  22.5 us (20%)
  local copies, waits for them, and re-layouts  12.2 us (11%)
  matrix products  2.09 us (2%)
  between operations  1.12 us (1%)
    ppermute x18, starting transfers between devices, flipped(): return lax.ppermute(value, axis, [(i, i ^ bit) for i in range(length)])  27 us
    ppermute x18, waiting for transfers between devices, flipped(): return lax.ppermute(value, axis, [(i, i ^ bit) for i in range(length)])  22.4 us
    unnamed x16, local copies, waits for them, and re-layouts  12.1 us
    pallas_call x2, Pallas kernels, other_sums(): pl.pallas_call(functools.partial(other_kernel, slots), out_shape=jax.Shap...  8.41 us
    ppermute x2, starting transfers between devices, whole_step(): arrived.append(lax.ppermute(outgoing, both, rim_pairs))  7.93 us
    pallas_call x2, Pallas kernels, rim_sums(): pl.pallas_call(functools.partial(rim_kernel, order), out_shape=(jax.Shape...  7.52 us
    pallas_call x1, Pallas kernels, own_sums(): pl.pallas_call(own_kernel, out_shape=(jax.ShapeDtypeStruct((annot.shape[0...  7.18 us
    pallas_call x1, Pallas kernels, gram_inverse(): pl.pallas_call(functools.partial(inverse_kernel, divisor), out_shape=(squ...  6.54 us
  transfers between devices with their start and end apart: 22, of which 10 were waited for; matrix products, arithmetic and copies ran while one was open for 1% of the time, Pallas kernels for 28%

commit v1 on v0

--- a/solution.py
+++ b/solution.py
@@ -293,19 +293,23 @@
 
 
 def rim_kernel(
-    order, n_ref, arrived_ref, turned_ref, annot_ref, sums_in, sums_ref, back_ref, geno, wide_values
+    order, n_ref, arrived_ref, turned_ref, annot_ref, sums_in, *refs
 ):
+    *earlier, sums_ref, back_ref, geno, wide_values = refs
+    columns = slice(order * TILE, (order + 1) * TILE)
     mine = turned_ref.shape[0]
     samples = geno.shape[1]
     n = n_ref[0]
     sums_ref[...] = sums_in[...]
     back_ref[...] = jnp.zeros_like(back_ref)
+    for ref in earlier:
+        back_ref[:, : ref.shape[1]] = ref[...]
     standardized(lambda rows: arrived_ref[rows, :], into(geno, 0), wide_values, samples)
 
     def add(y, inside=None):
         weights = band_weights(rows_of(turned_ref, y), columns_of(geno, 0), inside)
         sums_ref[:, cols_at(y)] += along_columns(arrived_ref[samples:, :], weights)
-        back_ref[...] += along_rows(annot_ref[:, cols_at(n * mine + y)], weights)
+        back_ref[:, columns] += along_rows(annot_ref[:, cols_at(n * mine + y)], weights)
 
     low, high = order, mine - 1 - order
     add((1 - n) * high + n * low, (1 - 2 * n) * tile_offset() <= 0)
@@ -320,16 +324,16 @@
                 add(y)
 
 
-def rim_sums(order, n, arrived, turned, annot, sums):
+def rim_sums(order, n, arrived, turned, annot, sums, *earlier):
     mine, chunks, _, _ = turned.shape
     samples = chunks * LANES
     return pl.pallas_call(
         functools.partial(rim_kernel, order),
         out_shape=(
             jax.ShapeDtypeStruct(sums.shape, jnp.float32),
-            jax.ShapeDtypeStruct((sums.shape[0], TILE), jnp.float32),
-        ),
-        in_specs=[in_smem] + [in_vmem] * 4,
+            jax.ShapeDtypeStruct((sums.shape[0], (order + 1) * TILE), jnp.float32),
+        ),
+        in_specs=[in_smem] + [in_vmem] * (4 + len(earlier)),
         out_specs=(in_vmem, in_vmem),
         scratch_shapes=[
             pltpu.VMEM((2, samples, LANES), jnp.bfloat16),
@@ -342,7 +346,7 @@
             transcendentals=0,
         ),
         name="rim_sums",
-    )(n, arrived, turned, annot, sums)
+    )(n, arrived, turned, annot, sums, *earlier)
 
 
 def eye(size):
@@ -362,15 +366,17 @@
     )
 
 
-def moments_kernel(total_variants, n_ref, w_ref, counts_ref, sums_ref, first_ref, second_ref, scores_ref, payload_ref, whole):
+def moments_kernel(total_variants, n_ref, w_ref, counts_ref, sums_ref, back_ref, scores_ref, payload_ref, whole):
     annots = counts_ref.shape[1]
     block = sums_ref.shape[1]
     mine = block // TILE
     n = n_ref[0]
     slot = 2 * w_ref[0] + n
     whole[...] = sums_ref[...]
-    for order, back_ref in enumerate((first_ref, second_ref)):
-        whole[:, cols_at((1 - n) * order + n * (mine - 1 - order))] += back_ref[...]
+    for order in range(back_ref.shape[1] // TILE):
+        whole[:, cols_at((1 - n) * order + n * (mine - 1 - order))] += back_ref[
+            :, order * TILE : (order + 1) * TILE
+        ]
     shares = upright(counts_ref[...]) / total_variants
     high = (1.0 - shares).astype(jnp.bfloat16).astype(jnp.float32)
     low = (0.0 - shares).astype(jnp.bfloat16).astype(jnp.float32)
@@ -402,7 +408,7 @@
             jax.ShapeDtypeStruct((annots + 2 * PAD, block), jnp.float32),
             jax.ShapeDtypeStruct((annots + slots, annots), jnp.float32),
         ),
-        in_specs=[in_smem] * 2 + [in_vmem] * 4,
+        in_specs=[in_smem] * 2 + [in_vmem] * 3,
         out_specs=(in_vmem, in_vmem),
         scratch_shapes=[pltpu.VMEM(sums.shape, jnp.float32)],
         compiler_params=pltpu.CompilerParams(vmem_limit_bytes=VMEM_LIMIT),
@@ -410,7 +416,7 @@
             flops=12 * annots * annots * block, bytes_accessed=12 * annots * block, transcendentals=0
         ),
         name="moments",
-    )(n, w, counts, sums, *back)
+    )(n, w, counts, sums, back)
 
 
 def inverse_kernel(divisor, payload_ref, inverse_ref, moments_ref):
@@ -653,12 +659,13 @@
     counts = wide_sum(counts)
     sums, turned = own_sums(n_array, dosage, annot)
     tiles = block // TILE
-    pieces = tuple(range(tiles // 2)), tuple(range(tiles // 2, tiles))
+    pieces = tuple(range(tiles // 4)), tuple(range(tiles // 4, tiles))
     back = []
     for order in range(2):
-        sums, part = rim_sums(order, n_array, arrived[order], turned, annot, sums)
-        back.append(lax.ppermute(part, both, back_pairs))
+        sums, part = rim_sums(order, n_array, arrived[order], turned, annot, sums, *back)
+        back.append(part)
         sums = other_sums(pieces[order], n_array, dosage, annot, turned, sums)
+    back = lax.ppermute(part, both, back_pairs)
 
     w_array = jnp.reshape(w, (1,)).astype(jnp.int32)
     extended, payload = moments_of(total_variants, 2 * wide, n_array, w_array, counts, sums, back)

time: 112 us -> 112 us (level)
  starting transfers between devices: 36.5 us -> 32.2 us
  local copies, waits for them, and re-layouts: 12.2 us -> 15.6 us
    ppermute x18, starting transfers between devices: 27 us -> 23.6 us  [flipped(): return lax.ppermute(value, axis, [(i, i ^ bit) for i in range(length)])]
    unnamed x16, local copies, waits for them, and re-layouts: 12.1 us -> 15.5 us
  transfers between devices with their start and end apart: 22 -> 21, of which waited for: 10 -> 10; matrix products, arithmetic and copies ran while one was open for 1% -> 1% of each run, Pallas kernels for 28% -> 28%
where the time goes in v1:
time: 112 us; the launch traced here: 111 us
  Pallas kernels  37.1 us (33%)
  starting transfers between devices  32.2 us (29%)
  waiting for transfers between devices  23.2 us (21%)
  local copies, waits for them, and re-layouts  15.6 us (14%)
  matrix products  2.09 us (2%)
    ppermute x18, starting transfers between devices, flipped(): return lax.ppermute(value, axis, [(i, i ^ bit) for i in range(length)])  23.6 us
    ppermute x18, waiting for transfers between devices, flipped(): return lax.ppermute(value, axis, [(i, i ^ bit) for i in range(length)])  23.2 us
    unnamed x16, local copies, waits for them, and re-layouts  15.5 us
    pallas_call x2, Pallas kernels, other_sums(): pl.pallas_call(functools.partial(other_kernel, slots), out_shape=jax.Shap...  8.31 us
    ppermute x2, starting transfers between devices, whole_step(): arrived.append(lax.ppermute(outgoing, both, rim_pairs))  7.93 us
    pallas_call x2, Pallas kernels, rim_sums(): pl.pallas_call(functools.partial(rim_kernel, order), out_shape=(jax.Shape...  7.52 us
    pallas_call x1, Pallas kernels, own_sums(): pl.pallas_call(own_kernel, out_shape=(jax.ShapeDtypeStruct((annot.shape[0...  7.18 us
    pallas_call x1, Pallas kernels, gram_inverse(): pl.pallas_call(functools.partial(inverse_kernel, divisor), out_shape=(squ...  6.54 us
  transfers between devices with their start and end apart: 21, of which 10 were waited for; matrix products, arithmetic and copies ran while one was open for 1% of the time, Pallas kernels for 28%

profile of v1, /device:TPU:0, one launch (start us, length us, event | category | flops | bytes accessed | tf_op | source)
XLA Modules:
  0.0 111.4 jit_solution(15777437370602004983)
XLA Ops:
  0.6 3.2 %outgoing.1 = (bf16[2184,256]{1,0:T(8,128)(2,1)}, bf16[2184,256]{1,0:T(8,128)(2,1)}) custom-call(s32[1]{0:T(128)} %bitcast.n_ref, bf16[2048,2048]{1,0:T(8,128)(2,1)} %dosage_ref.7, s32[128,2048]{1,0:T(8,128)} %annot_ref.3), custom_call_target="tpu_custom_call" | custom-call | bytes 4194304 | tf_op jit(solution)/shard_map/outgoing/pallas_call | solution.py:132
  3.9 3.4 %collective-permute-start.5 = (bf16[2184,256]{1,0:T(8,128)(2,1)}, bf16[2184,256]{1,0:T(8,128)(2,1)}, u32[]{:S(2)}, u32[]{:S(2)}) collective-permute-start(bf16[2184,256]{1,0:T(8,128)(2,1)} %get-tuple-element.21), channel_id=1, source_target_pairs={{0,2},{3,1},{2,4},{5,3},{4,6},{7,5},{6,8},{9,7},{8,10},{11,9},{10,... | collective-permute-start | bytes 3354632 | tf_op jit(solution)/shard_map/ppermute | solution.py:656
  7.3 4.5 %collective-permute-start.4 = (bf16[2184,256]{1,0:T(8,128)(2,1)}, bf16[2184,256]{1,0:T(8,128)(2,1)}, u32[]{:S(2)}, u32[]{:S(2)}) collective-permute-start(bf16[2184,256]{1,0:T(8,128)(2,1)} %get-tuple-element.20), channel_id=1, source_target_pairs={{0,2},{3,1},{2,4},{5,3},{4,6},{7,5},{6,8},{9,7},{8,10},{11,9},{10,... | collective-permute-start | bytes 3354632 | tf_op jit(solution)/shard_map/ppermute | solution.py:656
  11.8 1.2 %copy-done.7 = s32[128,2048]{1,0:T(8,128)S(1)} copy-done((s32[128,2048]{1,0:T(8,128)S(1)}, s32[128,2048]{1,0:T(8,128)}, u32[]{:S(2)}) %copy-start.7) | copy-done | bytes 1048600
  13.0 1.3 %prepare.1 = (bf16[136,2048]{1,0:T(8,128)(2,1)S(1)}, f32[1,128]{1,0:T(1,128)S(1)}, f32[1024,256]{1,0:T(8,128)}) custom-call(s32[1]{0:T(128)} %bitcast.n_ref, s32[128,2048]{1,0:T(8,128)S(1)} %copy-done.7, f32[2048,256]{1,0:T(8,128)S(1)} %copy-done.6), custom_call_target="tpu_custom_call" | custom-call | bytes 4194304 | tf_op jit(solution)/shard_map/prepare/pallas_call | solution.py:162
  14.3 0.1 collective-permute-start
  14.4 0.1 collective-permute-start.13
  14.5 0.0 copy-start.3
  14.5 3.4 %copy-done.3 = bf16[2048,2048]{1,0:T(8,128)(2,1)S(1)} copy-done((bf16[2048,2048]{1,0:T(8,128)(2,1)S(1)}, bf16[2048,2048]{1,0:T(8,128)(2,1)}, u32[]{:S(2)}) %copy-start.3) | copy-done | bytes 8388632
  17.9 7.2 %own_sums.1 = (f32[136,1024]{1,0:T(8,128)S(1)}, bf16[4,16,256,128]{3,2,1,0:T(8,128)(2,1)S(1)}) custom-call(s32[1]{0:T(128)} %bitcast.n_ref, bf16[2048,2048]{1,0:T(8,128)(2,1)S(1)} %copy-done.3, bf16[136,2048]{1,0:T(8,128)(2,1)S(1)} %get-tuple-element.18.annot_ref), custom_call_target="tpu_custom_call" | custom-call | flops 4294967296 | bytes 8388608 | tf_op jit(solution)/shard_map/own_sums/pallas_call | solution.py:252
  25.1 2.0 %copy-done = bf16[4,16,256,128]{3,2,1,0:T(8,128)(2,1)} copy-done((bf16[4,16,256,128]{3,2,1,0:T(8,128)(2,1)}, bf16[4,16,256,128]{3,2,1,0:T(8,128)(2,1)S(1)}, u32[]{:S(2)}) %copy-start) | copy-done | bytes 4194328
  27.0 2.0 %collective-permute-start.1 = (f32[1,128]{1,0:T(1,128)S(1)}, f32[1,128]{1,0:T(1,128)S(1)}, u32[]{:S(2)}, u32[]{:S(2)}) collective-permute-start(f32[1,128]{1,0:T(1,128)S(1)} %added.4.first_ref), channel_id=1, source_target_pairs={{0,8},{2,10},{4,12},{6,14},{8,0},{10,2},{12,4},{14,6},{16,24},{18,... | collective-permute-start | bytes 1544 | tf_op jit(solution)/shard_map/ppermute | solution.py:583
  29.0 1.6 %collective-permute-done.1.second_ref = f32[1,128]{1,0:T(1,128)S(1)} collective-permute-done((f32[1,128]{1,0:T(1,128)S(1)}, f32[1,128]{1,0:T(1,128)S(1)}, u32[]{:S(2)}, u32[]{:S(2)}) %collective-permute-start.1) | collective-permute-done | bytes 544 | tf_op jit(solution)/shard_map/ppermute | solution.py:583
  30.6 3.0 %collective-permute-start.2 = (f32[1,128]{1,0:T(1,128)S(1)}, f32[1,128]{1,0:T(1,128)S(1)}, u32[]{:S(2)}, u32[]{:S(2)}) collective-permute-start(f32[1,128]{1,0:T(1,128)S(1)} %added.5.first_ref), channel_id=1, source_target_pairs={{0,16},{2,18},{4,20},{6,22},{8,24},{10,26},{12,28},{14,30},{16,0},... | collective-permute-start | bytes 1544 | tf_op jit(solution)/shard_map/ppermute | solution.py:583
  33.6 1.5 %collective-permute-done.2.second_ref = f32[1,128]{1,0:T(1,128)S(1)} collective-permute-done((f32[1,128]{1,0:T(1,128)S(1)}, f32[1,128]{1,0:T(1,128)S(1)}, u32[]{:S(2)}, u32[]{:S(2)}) %collective-permute-start.2) | collective-permute-done | bytes 544 | tf_op jit(solution)/shard_map/ppermute | solution.py:583
  35.1 1.4 %collective-permute-start.3 = (f32[1,128]{1,0:T(1,128)S(1)}, f32[1,128]{1,0:T(1,128)S(1)}, u32[]{:S(2)}, u32[]{:S(2)}) collective-permute-start(f32[1,128]{1,0:T(1,128)S(1)} %added.6.first_ref), channel_id=1, source_target_pairs={{0,4},{2,6},{4,0},{6,2},{8,12},{10,14},{12,8},{14,10},{16,20},{18,... | collective-permute-start | bytes 1544 | tf_op jit(solution)/shard_map/ppermute | solution.py:583
  36.5 2.2 %collective-permute-done.3.second_ref = f32[1,128]{1,0:T(1,128)S(1)} collective-permute-done((f32[1,128]{1,0:T(1,128)S(1)}, f32[1,128]{1,0:T(1,128)S(1)}, u32[]{:S(2)}, u32[]{:S(2)}) %collective-permute-start.3) | collective-permute-done | bytes 544 | tf_op jit(solution)/shard_map/ppermute | solution.py:583
  38.7 2.2 %copy-done.1 = bf16[4,16,256,128]{3,2,1,0:T(8,128)(2,1)S(1)} copy-done((bf16[4,16,256,128]{3,2,1,0:T(8,128)(2,1)S(1)}, bf16[4,16,256,128]{3,2,1,0:T(8,128)(2,1)}, u32[]{:S(2)}) %copy-start.1) | copy-done | bytes 4194328
  40.9 5.1 %rim_sums.2 = (f32[136,1024]{1,0:T(8,128)S(1)}, f32[136,256]{1,0:T(8,128)S(1)}) custom-call(s32[1]{0:T(128)} %bitcast.n_ref, bf16[2184,256]{1,0:T(8,128)(2,1)} %collective-permute-done.5.arrived_ref, bf16[4,16,256,128]{3,2,1,0:T(8,128)(2,1)S(1)} %copy-done.1, bf16[136,2048]{1,0:T(8,128)(2,1)S(1)} %get-tuple-element.18.annot_ref, ...), custom_call_target="tpu_custom_call" | custom-call | flops 1073741824 | bytes 5242880 | tf_op jit(solution)/shard_map/rim_sums/pallas_call | solution.py:330
  46.0 0.0 copy-start.4
  46.0 3.4 %copy-done.4 = bf16[2048,2048]{1,0:T(8,128)(2,1)S(1)} copy-done((bf16[2048,2048]{1,0:T(8,128)(2,1)S(1)}, bf16[2048,2048]{1,0:T(8,128)(2,1)}, u32[]{:S(2)}) %copy-start.4) | copy-done | bytes 8388632
  49.4 3.4 %other_sums.2.sums_in = f32[136,1024]{1,0:T(8,128)S(1)} custom-call(s32[1]{0:T(128)} %bitcast.n_ref, bf16[2048,2048]{1,0:T(8,128)(2,1)S(1)} %copy-done.4, bf16[136,2048]{1,0:T(8,128)(2,1)S(1)} %get-tuple-element.18.annot_ref, bf16[4,16,256,128]{3,2,1,0:T(8,128)(2,1)S(1)} %copy-done.2, f32[136,1024]{1,0:T(8,128)S(1)} %get-tuple-element.23.sums_in), custom_call_target="tpu_custom_call" | custom-call | flops 4294967296 | bytes 8388608 | tf_op jit(solution)/shard_map/other_sums/pallas_call | solution.py:268
  52.8 2.5 %rim_sums.3 = (f32[136,1024]{1,0:T(8,128)S(1)}, f32[136,512]{1,0:T(8,128)S(1)}) custom-call(s32[1]{0:T(128)} %bitcast.n_ref, bf16[2184,256]{1,0:T(8,128)(2,1)} %collective-permute-done.4.arrived_ref, bf16[4,16,256,128]{3,2,1,0:T(8,128)(2,1)S(1)} %copy-done.2, bf16[136,2048]{1,0:T(8,128)(2,1)S(1)} %get-tuple-element.18.annot_ref, ...), custom_call_target="tpu_custom_call" | custom-call | flops 1073741824 | bytes 5242880 | tf_op jit(solution)/shard_map/rim_sums/pallas_call | solution.py:330
  55.2 0.7 collective-permute-start.6
  55.9 3.4 %copy-done.5 = bf16[2048,2048]{1,0:T(8,128)(2,1)S(1)} copy-done((bf16[2048,2048]{1,0:T(8,128)(2,1)S(1)}, bf16[2048,2048]{1,0:T(8,128)(2,1)}, u32[]{:S(2)}) %copy-start.5) | copy-done | bytes 8388632
  59.3 4.9 %other_sums.3.sums_ref = f32[136,1024]{1,0:T(8,128)S(1)} custom-call(s32[1]{0:T(128)} %bitcast.n_ref, bf16[2048,2048]{1,0:T(8,128)(2,1)S(1)} %copy-done.5, bf16[136,2048]{1,0:T(8,128)(2,1)S(1)} %get-tuple-element.18.annot_ref, bf16[4,16,256,128]{3,2,1,0:T(8,128)(2,1)S(1)} %copy-done.2, f32[136,1024]{1,0:T(8,128)S(1)} %get-tuple-element.25.sums_in), custom_call_target="tpu_custom_call" | custom-call | flops 4294967296 | bytes 8388608 | tf_op jit(solution)/shard_map/other_sums/pallas_call | solution.py:268
  64.3 0.9 moments.1
  65.1 0.4 fusion
  65.6 1.7 %fusion.6 = f32[144,256]{1,0:T(8,128)S(1)} fusion(f32[144,1024]{1,0:T(8,128)S(1)} %get-tuple-element.30.scores_ref, f32[1024,256]{1,0:T(8,128)} %collective-permute-done.13), kind=kOutput, calls=%fused_computation.15 | convolution fusion | flops 226492416 | bytes 1785856 | tf_op jit(solution)/shard_map/dot_general | solution.py:679
  67.3 7.6 %collective-permute-start.14 = (f32[72,512]{1,0:T(8,128)S(1)}, f32[72,512]{1,0:T(8,128)S(1)}, u32[]{:S(2)}, u32[]{:S(2)}) collective-permute-start(f32[72,512]{1,0:T(8,128)S(1)} %fusion.2), channel_id=1, source_target_pairs={{0,2},{2,0},{4,6},{6,4},{8,10},{10,8},{12,14},{14,12},{16,18},{18,... | collective-permute-start | bytes 442376 | tf_op jit(solution)/shard_map/ppermute | solution.py:583
  74.9 0.1 collective-permute-start.7
  75.0 0.9 collective-permute-done.14
  75.9 0.3 collective-permute-start.15
  76.3 1.8 %collective-permute-start.8 = (f32[80,128]{1,0:T(8,128)S(1)}, f32[80,128]{1,0:T(8,128)S(1)}, u32[]{:S(2)}, u32[]{:S(2)}) collective-permute-start(f32[80,128]{1,0:T(8,128)S(1)} %dynamic-slice_add_fusion), channel_id=1, source_target_pairs={{0,1},{1,0},{2,3},{3,2},{4,5},{5,4},{6,7},{7,6},{8,9},{9,8},{10,11... | collective-permute-start | bytes 122888 | tf_op jit(solution)/shard_map/ppermute | solution.py:583
  78.1 3.3 %collective-permute-done.8 = f32[80,128]{1,0:T(8,128)S(1)} collective-permute-done((f32[80,128]{1,0:T(8,128)S(1)}, f32[80,128]{1,0:T(8,128)S(1)}, u32[]{:S(2)}, u32[]{:S(2)}) %collective-permute-start.8) | collective-permute-done | bytes 40992 | tf_op jit(solution)/shard_map/ppermute | solution.py:583
  81.5 2.1 %collective-permute-start.16 = (f32[72,256]{1,0:T(8,128)S(1)}, f32[72,256]{1,0:T(8,128)S(1)}, u32[]{:S(2)}, u32[]{:S(2)}) collective-permute-start(f32[72,256]{1,0:T(8,128)S(1)} %slice_add_fusion), channel_id=1, source_target_pairs={{0,4},{2,6},{4,0},{6,2},{8,12},{10,14},{12,8},{14,10},{16,20},{18,... | collective-permute-start | bytes 221192 | tf_op jit(solution)/shard_map/ppermute | solution.py:583
  83.5 1.9 %collective-permute-done.9 = f32[80,128]{1,0:T(8,128)S(1)} collective-permute-done((f32[80,128]{1,0:T(8,128)S(1)}, f32[80,128]{1,0:T(8,128)S(1)}, u32[]{:S(2)}, u32[]{:S(2)}) %collective-permute-start.9) | collective-permute-done | bytes 40992 | tf_op jit(solution)/shard_map/ppermute | solution.py:583
  85.4 4.0 %collective-permute-done.10 = f32[80,128]{1,0:T(8,128)S(1)} collective-permute-done((f32[80,128]{1,0:T(8,128)S(1)}, f32[80,128]{1,0:T(8,128)S(1)}, u32[]{:S(2)}, u32[]{:S(2)}) %collective-permute-start.10) | collective-permute-done | bytes 40992 | tf_op jit(solution)/shard_map/ppermute | solution.py:583
  89.5 2.6 %collective-permute-start.11 = (f32[80,128]{1,0:T(8,128)S(1)}, f32[80,128]{1,0:T(8,128)S(1)}, u32[]{:S(2)}, u32[]{:S(2)}) collective-permute-start(f32[80,128]{1,0:T(8,128)S(1)} %add.58), channel_id=1, source_target_pairs={{0,16},{2,18},{4,20},{6,22},{8,24},{10,26},{12,28},{14,30},{16,0},... | collective-permute-start | bytes 122888 | tf_op jit(solution)/shard_map/ppermute | solution.py:583
  92.1 0.1 collective-permute-start.17
  92.2 2.2 %collective-permute-done.11 = f32[80,128]{1,0:T(8,128)S(1)} collective-permute-done((f32[80,128]{1,0:T(8,128)S(1)}, f32[80,128]{1,0:T(8,128)S(1)}, u32[]{:S(2)}, u32[]{:S(2)}) %collective-permute-start.11) | collective-permute-done | bytes 40992 | tf_op jit(solution)/shard_map/ppermute | solution.py:583
  94.4 0.8 collective-permute-start.20
  95.2 1.3 %collective-permute-done.17 = f32[72,256]{1,0:T(8,128)S(1)} collective-permute-done((f32[72,256]{1,0:T(8,128)S(1)}, f32[72,256]{1,0:T(8,128)S(1)}, u32[]{:S(2)}, u32[]{:S(2)}) %collective-permute-start.17) | collective-permute-done | bytes 73760 | tf_op jit(solution)/shard_map/ppermute | solution.py:583
  96.5 1.7 %collective-permute-start.18 = (f32[72,256]{1,0:T(8,128)S(1)}, f32[72,256]{1,0:T(8,128)S(1)}, u32[]{:S(2)}, u32[]{:S(2)}) collective-permute-start(f32[72,256]{1,0:T(8,128)S(1)} %add.66), channel_id=1, source_target_pairs={{0,16},{2,18},{4,20},{6,22},{8,24},{10,26},{12,28},{14,30},{16,0},... | collective-permute-start | bytes 221192 | tf_op jit(solution)/shard_map/ppermute | solution.py:583
  98.2 4.2 %collective-permute-done.18 = f32[72,256]{1,0:T(8,128)S(1)} collective-permute-done((f32[72,256]{1,0:T(8,128)S(1)}, f32[72,256]{1,0:T(8,128)S(1)}, u32[]{:S(2)}, u32[]{:S(2)}) %collective-permute-start.18) | collective-permute-done | bytes 73760 | tf_op jit(solution)/shard_map/ppermute | solution.py:583
  102.4 0.1 collective-permute-start.19
  102.5 6.5 %gram_inverse.1 = (f32[128,128]{1,0:T(8,128)S(1)}, f32[128,128]{1,0:T(8,128)S(1)}) custom-call(f32[160,128]{1,0:T(8,128)S(1)} %maximum_select_fusion.1.payload_ref), custom_call_target="tpu_custom_call" | custom-call | flops 20000000000 | bytes 65536 | tf_op jit(solution)/shard_map/gram_inverse/pallas_call | solution.py:498
  109.1 2.1 %fitted_values.1 = (f32[128,1024]{1,0:T(8,128)}, f32[2048,256]{1,0:T(8,128)}) custom-call(s32[1]{0:T(128)} %bitcast.n_ref, f32[128,128]{1,0:T(8,128)S(1)} %get-tuple-element.28.inverse_ref, f32[128,128]{1,0:T(8,128)S(1)} %get-tuple-element.29.moments_ref, f32[144,256]{1,0:T(8,128)S(1)} %maximum_select_fusion.proj_ref, ...), custom_call_target="tpu_custom_call" | custom-call | flops 134217728 | bytes 2097152 | tf_op jit(solution)/shard_map/fitted_values/pallas_call | solution.py:560
  (42 shorter events, 0.3 us)
Async XLA Ops:
  0.6 11.2 %copy-start.6 = (f32[2048,256]{1,0:T(8,128)S(1)}, f32[2048,256]{1,0:T(8,128)}, u32[]{:S(2)}) copy-start(f32[2048,256]{1,0:T(8,128)} %chi_ref.1) | copy-start | bytes 6291460
  3.9 34.9 %collective-permute-start.5 = (bf16[2184,256]{1,0:T(8,128)(2,1)}, bf16[2184,256]{1,0:T(8,128)(2,1)}, u32[]{:S(2)}, u32[]{:S(2)}) collective-permute-start(bf16[2184,256]{1,0:T(8,128)(2,1)} %get-tuple-element.21), channel_id=1, source_target_pairs={{0,2},{3,1},{2,4},{5,3},{4,6},{7,5},{6,8},{9,7},{8,10},{11,9},{10,... | collective-permute-start | bytes 3354632 | tf_op jit(solution)/shard_map/ppermute | solution.py:656
  7.3 45.5 %collective-permute-start.4 = (bf16[2184,256]{1,0:T(8,128)(2,1)}, bf16[2184,256]{1,0:T(8,128)(2,1)}, u32[]{:S(2)}, u32[]{:S(2)}) collective-permute-start(bf16[2184,256]{1,0:T(8,128)(2,1)} %get-tuple-element.20), channel_id=1, source_target_pairs={{0,2},{3,1},{2,4},{5,3},{4,6},{7,5},{6,8},{9,7},{8,10},{11,9},{10,... | collective-permute-start | bytes 3354632 | tf_op jit(solution)/shard_map/ppermute | solution.py:656
  11.8 1.2 %copy-start.7 = (s32[128,2048]{1,0:T(8,128)S(1)}, s32[128,2048]{1,0:T(8,128)}, u32[]{:S(2)}) copy-start(s32[128,2048]{1,0:T(8,128)} %annot_ref.3) | copy-start | bytes 3145732
  14.3 12.7 %collective-permute-start = (f32[1,128]{1,0:T(1,128)S(1)}, f32[1,128]{1,0:T(1,128)S(1)}, u32[]{:S(2)}, u32[]{:S(2)}) collective-permute-start(f32[1,128]{1,0:T(1,128)S(1)} %get-tuple-element.17.first_ref), channel_id=1, source_target_pairs={{0,2},{2,0},{4,6},{6,4},{8,10},{10,8},{12,14},{14,12},{16,18},{18,... | collective-permute-start | bytes 1544 | tf_op jit(solution)/shard_map/ppermute | solution.py:583
  14.4 51.2 %collective-permute-start.13 = (f32[1024,256]{1,0:T(8,128)}, f32[1024,256]{1,0:T(8,128)}, u32[]{:S(2)}, u32[]{:S(2)}) collective-permute-start(f32[1024,256]{1,0:T(8,128)} %get-tuple-element.31), channel_id=1, source_target_pairs={{0,1},{1,0},{2,3},{3,2},{4,5},{5,4},{6,7},{7,6},{8,9},{9,8},{10,11... | collective-permute-start | bytes 3145736 | tf_op jit(solution)/shard_map/ppermute | solution.py:583
  14.5 3.4 %copy-start.3 = (bf16[2048,2048]{1,0:T(8,128)(2,1)S(1)}, bf16[2048,2048]{1,0:T(8,128)(2,1)}, u32[]{:S(2)}) copy-start(bf16[2048,2048]{1,0:T(8,128)(2,1)} %dosage_ref.7) | copy-start | bytes 25165828
  25.1 2.0 %copy-start = (bf16[4,16,256,128]{3,2,1,0:T(8,128)(2,1)}, bf16[4,16,256,128]{3,2,1,0:T(8,128)(2,1)S(1)}, u32[]{:S(2)}) copy-start(bf16[4,16,256,128]{3,2,1,0:T(8,128)(2,1)S(1)} %get-tuple-element.19.turned_ref) | copy-start | bytes 12582916
  27.0 3.6 %collective-permute-start.1 = (f32[1,128]{1,0:T(1,128)S(1)}, f32[1,128]{1,0:T(1,128)S(1)}, u32[]{:S(2)}, u32[]{:S(2)}) collective-permute-start(f32[1,128]{1,0:T(1,128)S(1)} %added.4.first_ref), channel_id=1, source_target_pairs={{0,8},{2,10},{4,12},{6,14},{8,0},{10,2},{12,4},{14,6},{16,24},{18,... | collective-permute-start | bytes 1544 | tf_op jit(solution)/shard_map/ppermute | solution.py:583
  30.6 4.5 %collective-permute-start.2 = (f32[1,128]{1,0:T(1,128)S(1)}, f32[1,128]{1,0:T(1,128)S(1)}, u32[]{:S(2)}, u32[]{:S(2)}) collective-permute-start(f32[1,128]{1,0:T(1,128)S(1)} %added.5.first_ref), channel_id=1, source_target_pairs={{0,16},{2,18},{4,20},{6,22},{8,24},{10,26},{12,28},{14,30},{16,0},... | collective-permute-start | bytes 1544 | tf_op jit(solution)/shard_map/ppermute | solution.py:583
  35.1 3.6 %collective-permute-start.3 = (f32[1,128]{1,0:T(1,128)S(1)}, f32[1,128]{1,0:T(1,128)S(1)}, u32[]{:S(2)}, u32[]{:S(2)}) collective-permute-start(f32[1,128]{1,0:T(1,128)S(1)} %added.6.first_ref), channel_id=1, source_target_pairs={{0,4},{2,6},{4,0},{6,2},{8,12},{10,14},{12,8},{14,10},{16,20},{18,... | collective-permute-start | bytes 1544 | tf_op jit(solution)/shard_map/ppermute | solution.py:583
  38.7 2.2 %copy-start.1 = (bf16[4,16,256,128]{3,2,1,0:T(8,128)(2,1)S(1)}, bf16[4,16,256,128]{3,2,1,0:T(8,128)(2,1)}, u32[]{:S(2)}) copy-start(bf16[4,16,256,128]{3,2,1,0:T(8,128)(2,1)} %copy-done) | copy-start | bytes 12582916
  40.9 5.1 %copy-start.2 = (bf16[4,16,256,128]{3,2,1,0:T(8,128)(2,1)S(1)}, bf16[4,16,256,128]{3,2,1,0:T(8,128)(2,1)}, u32[]{:S(2)}) copy-start(bf16[4,16,256,128]{3,2,1,0:T(8,128)(2,1)} %copy-done) | copy-start | bytes 12582916
  46.0 3.4 %copy-start.4 = (bf16[2048,2048]{1,0:T(8,128)(2,1)S(1)}, bf16[2048,2048]{1,0:T(8,128)(2,1)}, u32[]{:S(2)}) copy-start(bf16[2048,2048]{1,0:T(8,128)(2,1)} %dosage_ref.7) | copy-start | bytes 25165828
  55.2 9.0 %collective-permute-start.6 = (f32[136,512]{1,0:T(8,128)S(1)}, f32[136,512]{1,0:T(8,128)S(1)}, u32[]{:S(2)}, u32[]{:S(2)}) collective-permute-start(f32[136,512]{1,0:T(8,128)S(1)} %get-tuple-element.26), channel_id=1, source_target_pairs={{1,2},{2,1},{3,4},{4,3},{5,6},{6,5},{7,8},{8,7},{9,10},{10,9},{11,... | collective-permute-start | bytes 835592 | tf_op jit(solution)/shard_map/ppermute | solution.py:668
  55.9 3.4 %copy-start.5 = (bf16[2048,2048]{1,0:T(8,128)(2,1)S(1)}, bf16[2048,2048]{1,0:T(8,128)(2,1)}, u32[]{:S(2)}) copy-start(bf16[2048,2048]{1,0:T(8,128)(2,1)} %dosage_ref.7) | copy-start | bytes 25165828
  67.3 8.6 %collective-permute-start.14 = (f32[72,512]{1,0:T(8,128)S(1)}, f32[72,512]{1,0:T(8,128)S(1)}, u32[]{:S(2)}, u32[]{:S(2)}) collective-permute-start(f32[72,512]{1,0:T(8,128)S(1)} %fusion.2), channel_id=1, source_target_pairs={{0,2},{2,0},{4,6},{6,4},{8,10},{10,8},{12,14},{14,12},{16,18},{18,... | collective-permute-start | bytes 442376 | tf_op jit(solution)/shard_map/ppermute | solution.py:583
  74.9 1.4 %collective-permute-start.7 = (f32[80,128]{1,0:T(8,128)S(1)}, f32[80,128]{1,0:T(8,128)S(1)}, u32[]{:S(2)}, u32[]{:S(2)}) collective-permute-start(f32[80,128]{1,0:T(8,128)S(1)} %constant_dynamic-slice_fusion), channel_id=1, source_target_pairs={{0,2},{2,0},{4,6},{6,4},{8,10},{10,8},{12,14},{14,12},{16,18},{18,... | collective-permute-start | bytes 122888 | tf_op jit(solution)/shard_map/ppermute | solution.py:583
  75.9 5.5 %collective-permute-start.15 = (f32[72,256]{1,0:T(8,128)S(1)}, f32[72,256]{1,0:T(8,128)S(1)}, u32[]{:S(2)}, u32[]{:S(2)}) collective-permute-start(f32[72,256]{1,0:T(8,128)S(1)} %slice.13), channel_id=1, source_target_pairs={{0,1},{1,0},{2,3},{3,2},{4,5},{5,4},{6,7},{7,6},{8,9},{9,8},{10,11... | collective-permute-start | bytes 221192 | tf_op jit(solution)/shard_map/ppermute | solution.py:583
  76.3 5.1 %collective-permute-start.8 = (f32[80,128]{1,0:T(8,128)S(1)}, f32[80,128]{1,0:T(8,128)S(1)}, u32[]{:S(2)}, u32[]{:S(2)}) collective-permute-start(f32[80,128]{1,0:T(8,128)S(1)} %dynamic-slice_add_fusion), channel_id=1, source_target_pairs={{0,1},{1,0},{2,3},{3,2},{4,5},{5,4},{6,7},{7,6},{8,9},{9,8},{10,11... | collective-permute-start | bytes 122888 | tf_op jit(solution)/shard_map/ppermute | solution.py:583
  81.4 4.0 %collective-permute-start.9 = (f32[80,128]{1,0:T(8,128)S(1)}, f32[80,128]{1,0:T(8,128)S(1)}, u32[]{:S(2)}, u32[]{:S(2)}) collective-permute-start(f32[80,128]{1,0:T(8,128)S(1)} %add.56), channel_id=1, source_target_pairs={{0,4},{2,6},{4,0},{6,2},{8,12},{10,14},{12,8},{14,10},{16,20},{18,... | collective-permute-start | bytes 122888 | tf_op jit(solution)/shard_map/ppermute | solution.py:583
  81.5 10.6 %collective-permute-start.16 = (f32[72,256]{1,0:T(8,128)S(1)}, f32[72,256]{1,0:T(8,128)S(1)}, u32[]{:S(2)}, u32[]{:S(2)}) collective-permute-start(f32[72,256]{1,0:T(8,128)S(1)} %slice_add_fusion), channel_id=1, source_target_pairs={{0,4},{2,6},{4,0},{6,2},{8,12},{10,14},{12,8},{14,10},{16,20},{18,... | collective-permute-start | bytes 221192 | tf_op jit(solution)/shard_map/ppermute | solution.py:583
  85.4 4.0 %collective-permute-start.10 = (f32[80,128]{1,0:T(8,128)S(1)}, f32[80,128]{1,0:T(8,128)S(1)}, u32[]{:S(2)}, u32[]{:S(2)}) collective-permute-start(f32[80,128]{1,0:T(8,128)S(1)} %add.57), channel_id=1, source_target_pairs={{0,8},{2,10},{4,12},{6,14},{8,0},{10,2},{12,4},{14,6},{16,24},{18,... | collective-permute-start | bytes 122888 | tf_op jit(solution)/shard_map/ppermute | solution.py:583
  89.5 4.9 %collective-permute-start.11 = (f32[80,128]{1,0:T(8,128)S(1)}, f32[80,128]{1,0:T(8,128)S(1)}, u32[]{:S(2)}, u32[]{:S(2)}) collective-permute-start(f32[80,128]{1,0:T(8,128)S(1)} %add.58), channel_id=1, source_target_pairs={{0,16},{2,18},{4,20},{6,22},{8,24},{10,26},{12,28},{14,30},{16,0},... | collective-permute-start | bytes 122888 | tf_op jit(solution)/shard_map/ppermute | solution.py:583
  92.1 4.4 %collective-permute-start.17 = (f32[72,256]{1,0:T(8,128)S(1)}, f32[72,256]{1,0:T(8,128)S(1)}, u32[]{:S(2)}, u32[]{:S(2)}) collective-permute-start(f32[72,256]{1,0:T(8,128)S(1)} %add.65), channel_id=1, source_target_pairs={{0,8},{2,10},{4,12},{6,14},{8,0},{10,2},{12,4},{14,6},{16,24},{18,... | collective-permute-start | bytes 221192 | tf_op jit(solution)/shard_map/ppermute | solution.py:583
  94.4 3.8 %collective-permute-start.12 = (f32[80,128]{1,0:T(8,128)S(1)}, f32[80,128]{1,0:T(8,128)S(1)}, u32[]{:S(2)}, u32[]{:S(2)}) collective-permute-start(f32[80,128]{1,0:T(8,128)S(1)} %add.59), channel_id=1, source_target_pairs={{0,2},{2,0},{4,6},{6,4},{8,10},{10,8},{12,14},{14,12},{16,18},{18,... | collective-permute-start | bytes 122888 | tf_op jit(solution)/shard_map/ppermute | solution.py:583
  94.4 14.7 %collective-permute-start.20 = (f32[128,1024]{1,0:T(8,128)S(1)}, f32[128,1024]{1,0:T(8,128)S(1)}, u32[]{:S(2)}, u32[]{:S(2)}) collective-permute-start(f32[128,1024]{1,0:T(8,128)S(1)} %slice.11), channel_id=1, source_target_pairs={{0,1},{1,0},{2,3},{3,2},{4,5},{5,4},{6,7},{7,6},{8,9},{9,8},{10,11... | collective-permute-start | bytes 1572872 | tf_op jit(solution)/shard_map/ppermute | solution.py:583
  96.5 5.9 %collective-permute-start.18 = (f32[72,256]{1,0:T(8,128)S(1)}, f32[72,256]{1,0:T(8,128)S(1)}, u32[]{:S(2)}, u32[]{:S(2)}) collective-permute-start(f32[72,256]{1,0:T(8,128)S(1)} %add.66), channel_id=1, source_target_pairs={{0,16},{2,18},{4,20},{6,22},{8,24},{10,26},{12,28},{14,30},{16,0},... | collective-permute-start | bytes 221192 | tf_op jit(solution)/shard_map/ppermute | solution.py:583
  102.4 6.6 %collective-permute-start.19 = (f32[72,256]{1,0:T(8,128)S(1)}, f32[72,256]{1,0:T(8,128)S(1)}, u32[]{:S(2)}, u32[]{:S(2)}) collective-permute-start(f32[72,256]{1,0:T(8,128)S(1)} %add.67), channel_id=1, source_target_pairs={{0,2},{2,0},{4,6},{6,4},{8,10},{10,8},{12,14},{14,12},{16,18},{18,... | collective-permute-start | bytes 221192 | tf_op jit(solution)/shard_map/ppermute | solution.py:583
